TPU v7x, 32 devices: a whole 2x2x4 slice. The times are simulated.
32 devices in a mesh: rows: 8 (over z, y), cols: 4 (over x, core).
Axes of the slice: x: 2, y: 2, z: 4, core: 2. Of those that a mesh axis runs over, the one named last changes fastest.
Arguments:
- snapshot: float32 [3072, 8192], P('rows', 'cols'), may hold values from -270 to 270
- test_matrix: float32 [8192, 256], P('cols'), may hold values from -0.0625 to 0.0625
Outputs:
- projected: float32 [8192, 256], P('cols')
- triangle: float32 [256, 256], replicated
All inputs are finite; a program needn't handle non-finite values.
Results may differ from a plain program's by a relative error of at most 0.00007.
Values sent between devices are 32-bit elements; how exact they have to be, the bound alone decides.
No kernel may reach another device: no remote copies, remote signals or barrier semaphores. Data moves between devices by JAX's collectives and lax.ppermute only.
A program may use at most 64 MiB of HBM per device.

v0:
```python
import functools

import jax
import jax.numpy as jnp
from jax import lax
from jax.experimental import pallas as pl
from jax.experimental.pallas import tpu as pltpu
from jax.sharding import PartitionSpec as P


high = lax.Precision.HIGHEST
VMEM = pl.BlockSpec(memory_space=pltpu.VMEM)
ANY = pl.BlockSpec(memory_space=pltpu.HBM)
F32, BF16 = jnp.float32, jnp.bfloat16
MIB = 1 << 20


def mm(left, right, dims, precision=high):
    return lax.dot_general(
        left, right, (dims, ((), ())), precision=precision, preferred_element_type=F32
    )


def split(value):
    top = value.astype(BF16)
    return top, (value - top.astype(F32)).astype(BF16)


def mm3(left, right, dims):
    def one(a, b):
        return lax.dot_general(a, b, (dims, ((), ())), preferred_element_type=F32)

    return one(left[0], right[0]) + (one(left[0], right[1]) + one(left[1], right[0]))


def array(shape, dtype=F32):
    return jax.ShapeDtypeStruct(shape, dtype)


def call(kernel, outs, *args, specs=None, out_specs=None, scratch=(), flops=0, vmem=8, **more):
    outs = tuple(outs)
    return pl.pallas_call(
        kernel,
        out_shape=outs,
        in_specs=specs or [VMEM] * len(args),
        out_specs=out_specs or (VMEM,) * len(outs),
        scratch_shapes=list(scratch),
        compiler_params=pltpu.CompilerParams(vmem_limit_bytes=vmem * MIB),
        cost_estimate=pl.CostEstimate(
            flops=flops,
            bytes_accessed=sum(a.size * a.dtype.itemsize for a in args),
            transcendentals=0,
        ),
        **more,
    )(*args)


def factor_kernel(block, top, gram_ref, *refs):
    *above, out_ref, part = refs
    panel, n = out_ref.shape[0], gram_ref.shape[0]
    row = lax.broadcasted_iota(jnp.int32, (panel, n), 0)
    col = lax.broadcasted_iota(jnp.int32, (panel, n), 1)
    sub = lax.broadcasted_iota(jnp.int32, (block, 2 * n), 0)
    lanes = min(n, 128)

    def wide(v):
        return jnp.concatenate([v] * (2 * n // lanes), axis=1)

    eye = jnp.where(row + top == col, 1.0, 0.0).astype(F32)
    rest = jnp.concatenate([gram_ref[top : top + panel, :], eye], axis=1)
    for ref in above:
        rest = rest - mm(ref[:, top : top + panel], ref[...], ((0,), (0,)))
    part[...] = rest
    for inner in range(0, panel, block):
        k = top + inner
        rows = part[inner : inner + block, :]
        columns = [
            jnp.broadcast_to(rows[:, k + j : k + j + 1], (block, lanes)) for j in range(block)
        ]
        d = {
            (i, j): jnp.broadcast_to(columns[j][i : i + 1, :], (block, lanes))
            for i in range(block)
            for j in range(i, block)
        }
        scale = []
        for i in range(block):
            scale.append(lax.rsqrt(d[i, i]))
            for j in range(i + 1, block):
                d[i, j] = d[i, j] * scale[i]
            for j in range(i + 1, block):
                for l in range(j, block):
                    d[j, l] = d[j, l] - d[i, j] * d[i, l]
        done, solved = [], jnp.zeros((block, 2 * n), F32)
        for i in range(block):
            line = jnp.broadcast_to(rows[i : i + 1, :], (block, 2 * n))
            for m in range(i):
                line = line - wide(d[m, i]) * done[m]
            line = line * wide(scale[i])
            done.append(line)
            solved = jnp.where(sub == i, line, solved)
        out_ref[inner : inner + block, :] = solved
        if inner + block < panel:
            part[inner + block :, :] -= mm(
                solved[:, k + block : top + panel], solved, ((0,), (0,))
            )


def factor_rows(gram, above):
    n = gram.shape[0]
    panel = min(n, 64)
    top = panel * len(above)
    (rows,) = call(
        functools.partial(factor_kernel, 8, top),
        [array((panel, 2 * n))],
        gram,
        *above,
        scratch=[pltpu.VMEM((panel, 2 * n), F32)],
        flops=12 * n**3 // 4,
    )
    return rows


def upper_part(panels):
    n = panels[0].shape[1] // 2
    whole = jnp.concatenate([p[:, :n] for p in panels])
    return jnp.triu(whole)


def lower_part(panels):
    n = panels[0].shape[1] // 2
    return jnp.concatenate([p[:, n:] for p in panels])


def sketch_kernel(axis, snap_any, test_any, mine_ref, other_ref, top_ref, rest_ref, snap, test, sems):
    depth = snap.shape[1]
    chunks = sems.shape[1]
    size = depth // chunks
    copies = []
    for c in range(chunks):
        part = pl.ds(c * size, size)
        copies.append(
            (
                pltpu.make_async_copy(snap_any.at[:, part], snap.at[:, part], sems.at[0, c]),
                pltpu.make_async_copy(test_any.at[part], test.at[part], sems.at[1, c]),
            )
        )
    for a, b in copies:
        b.start()
        a.start()
    total = None
    for c, (a, b) in enumerate(copies):
        b.wait()
        a.wait()
        part = slice(c * size, (c + 1) * size)
        left = split(snap[:, part])
        top_ref[:, part], rest_ref[:, part] = left
        term = mm3(left, split(test[part, :]), ((1,), (0,)))
        total = term if total is None else total + term
    half = total.shape[0] // 2
    first = lax.axis_index(axis) & 1
    low, high_ = total[:half], total[half:]
    mine_ref[...] = jnp.where(first == 0, low, high_)
    other_ref[...] = jnp.where(first == 0, high_, low)


def sketch_parts(snapshot, test_matrix, axis):
    points, depth = snapshot.shape
    width = test_matrix.shape[1]
    chunks = 4
    half = array((points // 2, width))
    return call(
        functools.partial(sketch_kernel, axis),
        (half, half, array(snapshot.shape, BF16), array(snapshot.shape, BF16)),
        pltpu.with_memory_space_constraint(snapshot, pltpu.HBM),
        pltpu.with_memory_space_constraint(test_matrix, pltpu.HBM),
        specs=[ANY, ANY],
        scratch=[
            pltpu.VMEM(snapshot.shape, F32),
            pltpu.VMEM(test_matrix.shape, F32),
            pltpu.SemaphoreType.DMA((2, chunks)),
        ],
        flops=6 * points * depth * width,
        vmem=24,
    )


def swap(value, axis, mask):
    return lax.ppermute(value, axis, [(i, i ^ mask) for i in range(lax.axis_size(axis))])


def first_bit(axis):
    return lax.axis_index(axis) & 1


def ordered(axis, mine, other):
    low = first_bit(axis) == 0
    return jnp.where(low, mine, other), jnp.where(low, other, mine)


def strip_kernel(axis, mine_ref, other_ref, out_ref, scratch):
    half = mine_ref.shape[0]
    bit = first_bit(axis)
    scratch[pl.ds(pl.multiple_of(bit * half, half), half), :] = mine_ref[...]
    scratch[pl.ds(pl.multiple_of((1 - bit) * half, half), half), :] = other_ref[...]
    width = out_ref.shape[1]
    left = scratch[:, pl.ds(pl.multiple_of(bit * width, width), width)]
    out_ref[:width, :] = mm(left, left, ((0,), (0,)))
    cross = mm(scratch[:, :width], scratch[:, width:], ((0,), (0,)))
    out_ref[width:, :] = jnp.where(bit == 0, cross[: width // 2], cross[width // 2 :])


def gram_part(mine, other, axis):
    half, width = mine.shape
    block = width // 2
    (out,) = call(
        functools.partial(strip_kernel, axis),
        [array((block + block // 2, block))],
        mine,
        other,
        scratch=[pltpu.VMEM((2 * half, width), F32)],
        flops=6 * half * width * width,
    )
    return out


def gram_upper(axis, mine, other):
    first, second = ordered(axis, mine, other)
    block = first.shape[1]
    cross = jnp.concatenate([first[block:], second[block:]])
    above = jnp.concatenate([first[:block], cross], axis=1)
    below = jnp.concatenate([jnp.zeros_like(cross), second[:block]], axis=1)
    return jnp.concatenate([above, below])


class Ring:
    def __init__(self, axis):
        self.axis = axis
        self.length = lax.axis_size(axis)

    def slab(self, ahead):
        index = lax.axis_index(self.axis)
        place = index >> 1
        here = jnp.where((index & 1) == 0, place, self.length - 1 - place)
        return lax.rem(here + (ahead % self.length), self.length)

    def row(self, position):
        n = self.length
        position %= n
        return 2 * position if 2 * position < n else 2 * (n - 1 - position) + 1

    def send(self, value, way):
        pairs = [(self.row(p), self.row(p + way)) for p in range(self.length)]
        return lax.ppermute(value, self.axis, pairs)


def product_kernel(ring, axis, aheads, first, *refs):
    if first:
        mine_ref, other_ref, top_ref, rest_ref, stop_ref, srest_ref, *outs = refs
        half = mine_ref.shape[0]
        bit = first_bit(axis)
        for ref, at in ((mine_ref, bit), (other_ref, 1 - bit)):
            where = pl.ds(pl.multiple_of(at * half, half), half)
            stop_ref[where, :], srest_ref[where, :] = split(ref[...])
    else:
        stop_ref, srest_ref, top_ref, rest_ref, *outs = refs
    right = (stop_ref[...], srest_ref[...])
    for ahead, out in zip(aheads, outs):
        size = out.shape[0]
        at = pl.ds(pl.multiple_of(ring.slab(ahead) * size, size), size)
        out[...] = mm3((top_ref[:, at], rest_ref[:, at]), right, ((0,), (0,)))


def products(ring, axis, aheads, first, one, two, top, rest):
    points, columns = top.shape
    width = one.shape[1]
    size = columns // ring.length
    outs = [array((size, width))] * len(aheads)
    if first:
        outs = [array((points, width), BF16)] * 2 + outs
    return call(
        functools.partial(product_kernel, ring, axis, aheads, first),
        outs,
        one,
        two,
        top,
        rest,
        flops=6 * points * width * size * len(aheads),
        vmem=12,
    )


def final_kernel(ring, places, panels, *refs):
    count = len(places)
    lower = refs[:panels]
    pieces, refs = refs[panels : panels + count], refs[panels + count :]
    out_any, held, sems = refs[-3:]
    n = held.shape[2]
    size = out_any.shape[0] // ring.length
    right = split(jnp.concatenate([ref[:, n:] for ref in lower]))
    copies = []
    for i, ((ahead, offset), piece) in enumerate(zip(places, pieces)):
        rows = piece.shape[0]
        held[i, :rows] = mm3(split(piece[...]), right, ((1,), (1,)))
        at = pl.ds(pl.multiple_of(ring.slab(ahead) * size + offset, rows), rows)
        copy = pltpu.make_async_copy(held.at[i, pl.ds(0, rows)], out_any.at[at], sems.at[i])
        copy.start()
        copies.append(copy)
    for copy in copies:
        copy.wait()


def final(ring, pieces, panels, size, before=None):
    width = panels[0].shape[1] // 2
    args = [*panels, *pieces.values()]
    specs = [VMEM] * len(args)
    more = {}
    if before is not None:
        more["input_output_aliases"] = {len(args): 0}
        args.append(before)
        specs.append(ANY)
    count = len(pieces)
    (out,) = call(
        functools.partial(final_kernel, ring, tuple(pieces), len(panels)),
        [array((size * ring.length, width))],
        *args,
        specs=specs,
        out_specs=(ANY,),
        scratch=[pltpu.VMEM((count, size, width), F32), pltpu.SemaphoreType.DMA((count,))],
        flops=6 * sum(p.shape[0] for p in pieces.values()) * width * width,
        **more,
    )
    return out


def body(snapshot, test_matrix):
    return steps(snapshot, test_matrix)


def steps(snapshot, test_matrix):
    mine, other, top, rest = sketch_parts(snapshot, test_matrix, "cols")
    columns = lax.axis_size("cols")
    mine = mine + swap(other, "cols", 1)
    mask = 2
    while mask < columns:
        mine = mine + swap(mine, "cols", mask)
        mask *= 2
    other = swap(mine, "cols", 1)

    ring = Ring("rows")
    far = ring.length // 2
    stop, srest, part = products(ring, "cols", [far], True, mine, other, top, rest)
    size = part.shape[0]
    half = size // 2
    right, left = part[:half], part[half:]
    right = ring.send(right, 1)
    left = ring.send(left, -1)
    strip = gram_part(mine, other, "cols")
    step = 1
    while step < ring.length:
        strip = strip + swap(strip, "rows", step)
        step *= 2
    gram = gram_upper("cols", strip, swap(strip, "cols", 1))
    aheads = [sign * d for d in range(far - 1, 0, -1) for sign in (1, -1)] + [0]
    parts = products(ring, "cols", aheads, False, stop, srest, top, rest)
    parts = dict(zip(aheads, parts))
    for d in range(far - 1, 0, -1):
        if d == far - 1:
            right = jnp.pad(right, ((0, half), (0, 0)))
            left = jnp.pad(left, ((half, 0), (0, 0)))
        right = ring.send(parts[d] + right, 1)
        left = ring.send(parts[-d] + left, -1)
    own = parts[0] + (right + left)
    panels = []
    while len(panels) * 64 < gram.shape[0]:
        panels.append(factor_rows(gram, panels))
    early, late = {(0, 0): own}, {}
    right = left = own
    for d in range(1, far + 1):
        if d == far:
            right, left = right[:half], left[half:]
        right = ring.send(right, 1)
        left = ring.send(left, -1)
        held = early if d < far else late
        held[-d, 0] = right
        held[d, half if d == far else 0] = left
    out = final(ring, early, panels, size)
    projected = final(ring, late, panels, size, out)
    total = snapshot.shape[0] * lax.axis_size("rows")
    return (projected, upper_part(panels) / jnp.sqrt(jnp.float32(total)))


def plain_body(snapshot, test_matrix):
    sketch = lax.psum(mm(snapshot, test_matrix, ((1,), (0,))), "cols")
    gram = lax.psum(mm(sketch, sketch, ((0,), (0,))), "rows")
    panels = []
    while len(panels) * 64 < gram.shape[0]:
        panels.append(factor_rows(gram, panels))
    product = lax.psum(mm(snapshot, sketch, ((0,), (0,))), "rows")
    total = snapshot.shape[0] * lax.axis_size("rows")
    projected = mm(product, lower_part(panels), ((1,), (1,)))
    return (projected, upper_part(panels) / jnp.sqrt(jnp.float32(total)))


def solution(mesh):
    rows = mesh.shape["rows"]
    ring = rows == 8
    return jax.shard_map(
        body if ring else plain_body,
        mesh=mesh,
        in_specs=(P("rows", "cols"), P("cols", None)),
        out_specs=(P("cols", None), P()),
        check_vma=False,
    )
```

profile of v0, /device:TPU:0, one launch (start us, length us, event | category | flops | bytes accessed | tf_op | source)
XLA Modules:
  0.0 95.1 jit_solution(6334675693359028531)
XLA Ops:
  0.6 4.3 %shard_map.41 = (f32[192,256]{1,0:T(8,128)S(1)}, f32[192,256]{1,0:T(8,128)S(1)}, bf16[384,2048]{1,0:T(8,128)(2,1)S(1)}, bf16[384,2048]{1,0:T(8,128)(2,1)S(1)}) custom-call(f32[384,2048]{1,0:T(8,128)} %snap_any.1, f32[2048,256]{1,0:T(8,128)} %test_any.1), custom_call_target="tpu_custom_call" | custom-call | flops 1207959552 | bytes 5242880 | tf_op jit(solution)/shard_map/pallas_call | solution.py:42
  6.6 2.9 %collective-permute-start.1 = (f32[192,256]{1,0:T(8,128)S(1)}, f32[192,256]{1,0:T(8,128)S(1)}, u32[]{:S(2)}, u32[]{:S(2)}) collective-permute-start(f32[192,256]{1,0:T(8,128)S(1)} %add.54), channel_id=1, source_target_pairs={{0,2},{1,3},{2,0},{3,1},{4,6},{5,7},{6,4},{7,5},{8,10},{9,11},{10,... | collective-permute-start | bytes 589832 | tf_op jit(solution)/shard_map/ppermute | solution.py:188
  9.5 5.2 %collective-permute-done.1 = f32[192,256]{1,0:T(8,128)S(1)} collective-permute-done((f32[192,256]{1,0:T(8,128)S(1)}, f32[192,256]{1,0:T(8,128)S(1)}, u32[]{:S(2)}, u32[]{:S(2)}) %collective-permute-start.1) | collective-permute-done | bytes 196640 | tf_op jit(solution)/shard_map/ppermute | solution.py:188
  16.7 1.9 %collective-permute-start.7 = (f32[128,256]{1,0:T(8,128)S(1)}, f32[128,256]{1,0:T(8,128)S(1)}, u32[]{:S(2)}, u32[]{:S(2)}) collective-permute-start(f32[128,256]{1,0:T(8,128)S(1)} %get-tuple-element.31), channel_id=1, source_target_pairs={{0,8},{8,16},{16,24},{24,28},{28,20},{20,12},{12,4},{4,0},{1,9},{9... | collective-permute-start | bytes 393224 | tf_op jit(solution)/shard_map/ppermute | solution.py:253
  20.5 1.9 %collective-permute-done.7 = f32[128,256]{1,0:T(8,128)S(1)} collective-permute-done((f32[128,256]{1,0:T(8,128)S(1)}, f32[128,256]{1,0:T(8,128)S(1)}, u32[]{:S(2)}, u32[]{:S(2)}) %collective-permute-start.7) | collective-permute-done | bytes 131104 | tf_op jit(solution)/shard_map/ppermute | solution.py:253
  22.4 1.8 %collective-permute-start.8 = (f32[256,256]{1,0:T(8,128)S(1)}, f32[256,256]{1,0:T(8,128)S(1)}, u32[]{:S(2)}, u32[]{:S(2)}) collective-permute-start(f32[256,256]{1,0:T(8,128)S(1)} %pad_add_fusion.1), channel_id=1, source_target_pairs={{0,8},{8,16},{16,24},{24,28},{28,20},{20,12},{12,4},{4,0},{1,9},{9... | collective-permute-start | bytes 786440 | tf_op jit(solution)/shard_map/ppermute | solution.py:253
  24.5 5.4 %collective-permute-done.8 = f32[256,256]{1,0:T(8,128)S(1)} collective-permute-done((f32[256,256]{1,0:T(8,128)S(1)}, f32[256,256]{1,0:T(8,128)S(1)}, u32[]{:S(2)}, u32[]{:S(2)}) %collective-permute-start.8) | collective-permute-done | bytes 262176 | tf_op jit(solution)/shard_map/ppermute | solution.py:253
  30.0 1.8 %collective-permute-start.9 = (f32[256,256]{1,0:T(8,128)S(1)}, f32[256,256]{1,0:T(8,128)S(1)}, u32[]{:S(2)}, u32[]{:S(2)}) collective-permute-start(f32[256,256]{1,0:T(8,128)S(1)} %add.60), channel_id=1, source_target_pairs={{0,8},{8,16},{16,24},{24,28},{28,20},{20,12},{12,4},{4,0},{1,9},{9... | collective-permute-start | bytes 786440 | tf_op jit(solution)/shard_map/ppermute | solution.py:253
  32.2 4.5 %collective-permute-done.9 = f32[256,256]{1,0:T(8,128)S(1)} collective-permute-done((f32[256,256]{1,0:T(8,128)S(1)}, f32[256,256]{1,0:T(8,128)S(1)}, u32[]{:S(2)}, u32[]{:S(2)}) %collective-permute-start.9) | collective-permute-done | bytes 262176 | tf_op jit(solution)/shard_map/ppermute | solution.py:253
  36.8 1.8 %collective-permute-start.10 = (f32[256,256]{1,0:T(8,128)S(1)}, f32[256,256]{1,0:T(8,128)S(1)}, u32[]{:S(2)}, u32[]{:S(2)}) collective-permute-start(f32[256,256]{1,0:T(8,128)S(1)} %add.61), channel_id=1, source_target_pairs={{0,8},{8,16},{16,24},{24,28},{28,20},{20,12},{12,4},{4,0},{1,9},{9... | collective-permute-start | bytes 786440 | tf_op jit(solution)/shard_map/ppermute | solution.py:253
  38.9 4.2 %collective-permute-done.10 = f32[256,256]{1,0:T(8,128)S(1)} collective-permute-done((f32[256,256]{1,0:T(8,128)S(1)}, f32[256,256]{1,0:T(8,128)S(1)}, u32[]{:S(2)}, u32[]{:S(2)}) %collective-permute-start.10) | collective-permute-done | bytes 262176 | tf_op jit(solution)/shard_map/ppermute | solution.py:253
  43.2 1.8 %collective-permute-done.14 = f32[256,256]{1,0:T(8,128)S(1)} collective-permute-done((f32[256,256]{1,0:T(8,128)S(1)}, f32[256,256]{1,0:T(8,128)S(1)}, u32[]{:S(2)}, u32[]{:S(2)}) %collective-permute-start.14) | collective-permute-done | bytes 262176 | tf_op jit(solution)/shard_map/ppermute | solution.py:253
  48.6 5.4 %collective-permute-done.3 = f32[192,128]{1,0:T(8,128)S(1)} collective-permute-done((f32[192,128]{1,0:T(8,128)S(1)}, f32[192,128]{1,0:T(8,128)S(1)}, u32[]{:S(2)}, u32[]{:S(2)}) %collective-permute-start.3) | collective-permute-done | bytes 98336 | tf_op jit(solution)/shard_map/ppermute | solution.py:188
  54.1 2.0 %collective-permute-start.16 = (f32[256,256]{1,0:T(8,128)S(1)}, f32[256,256]{1,0:T(8,128)S(1)}, u32[]{:S(2)}, u32[]{:S(2)}) collective-permute-start(f32[256,256]{1,0:T(8,128)S(1)} %collective-permute-done.15.refs_5_), channel_id=1, source_target_pairs={{0,8},{8,16},{16,24},{24,28},{28,20},{20,12},{12,4},{4,0},{1,9},{9... | collective-permute-start | bytes 786440 | tf_op jit(solution)/shard_map/ppermute | solution.py:253
  56.5 3.2 %collective-permute-done.4 = f32[192,128]{1,0:T(8,128)S(1)} collective-permute-done((f32[192,128]{1,0:T(8,128)S(1)}, f32[192,128]{1,0:T(8,128)S(1)}, u32[]{:S(2)}, u32[]{:S(2)}) %collective-permute-start.4) | collective-permute-done | bytes 98336 | tf_op jit(solution)/shard_map/ppermute | solution.py:188
  59.7 3.6 %collective-permute-start.5 = (f32[192,128]{1,0:T(8,128)S(1)}, f32[192,128]{1,0:T(8,128)S(1)}, u32[]{:S(2)}, u32[]{:S(2)}) collective-permute-start(f32[192,128]{1,0:T(8,128)S(1)} %add.57), channel_id=1, source_target_pairs={{0,16},{4,20},{8,24},{12,28},{16,0},{20,4},{24,8},{28,12},{1,17},{... | collective-permute-start | bytes 294920 | tf_op jit(solution)/shard_map/ppermute | solution.py:188
  63.3 5.8 %collective-permute-done.5 = f32[192,128]{1,0:T(8,128)S(1)} collective-permute-done((f32[192,128]{1,0:T(8,128)S(1)}, f32[192,128]{1,0:T(8,128)S(1)}, u32[]{:S(2)}, u32[]{:S(2)}) %collective-permute-start.5) | collective-permute-done | bytes 98336 | tf_op jit(solution)/shard_map/ppermute | solution.py:188
  69.3 2.0 %collective-permute-start.21 = (f32[256,256]{1,0:T(8,128)S(1)}, f32[256,256]{1,0:T(8,128)S(1)}, u32[]{:S(2)}, u32[]{:S(2)}) collective-permute-start(f32[256,256]{1,0:T(8,128)S(1)} %collective-permute-done.20.refs_8_), channel_id=1, source_target_pairs={{0,4},{8,0},{16,8},{24,16},{28,24},{20,28},{12,20},{4,12},{1,5},{9... | collective-permute-start | bytes 786440 | tf_op jit(solution)/shard_map/ppermute | solution.py:253
  71.4 3.8 %shard_map.43.refs_0_ = f32[64,512]{1,0:T(8,128)S(1)} custom-call(f32[256,256]{1,0:T(8,128)S(1)} %select_maximum_fusion.gram_ref), custom_call_target="tpu_custom_call" | custom-call | flops 50331648 | bytes 262144 | tf_op jit(solution)/shard_map/pallas_call | solution.py:42
  75.3 4.2 %shard_map.44.refs_1_ = f32[64,512]{1,0:T(8,128)S(1)} custom-call(f32[256,256]{1,0:T(8,128)S(1)} %select_maximum_fusion.gram_ref, f32[64,512]{1,0:T(8,128)S(1)} %shard_map.43.refs_0_), custom_call_target="tpu_custom_call" | custom-call | flops 50331648 | bytes 393216 | tf_op jit(solution)/shard_map/pallas_call | solution.py:42
  79.5 4.2 %shard_map.45.refs_2_ = f32[64,512]{1,0:T(8,128)S(1)} custom-call(f32[256,256]{1,0:T(8,128)S(1)} %select_maximum_fusion.gram_ref, f32[64,512]{1,0:T(8,128)S(1)} %shard_map.43.refs_0_, f32[64,512]{1,0:T(8,128)S(1)} %shard_map.44.refs_1_), custom_call_target="tpu_custom_call" | custom-call | flops 50331648 | bytes 524288 | tf_op jit(solution)/shard_map/pallas_call | solution.py:42
  83.7 4.4 %shard_map.46.refs_3_ = f32[64,512]{1,0:T(8,128)S(1)} custom-call(f32[256,256]{1,0:T(8,128)S(1)} %select_maximum_fusion.gram_ref, f32[64,512]{1,0:T(8,128)S(1)} %shard_map.43.refs_0_, f32[64,512]{1,0:T(8,128)S(1)} %shard_map.44.refs_1_, f32[64,512]{1,0:T(8,128)S(1)} %shard_map.45.refs_2_), custom_call_target="tpu_custom_call" | custom-call | flops 50331648 | bytes 655360 | tf_op jit(solution)/shard_map/pallas_call | solution.py:42
  88.5 1.8 %collective-permute-start.22 = (f32[128,256]{1,0:T(8,128)S(1)}, f32[128,256]{1,0:T(8,128)S(1)}, u32[]{:S(2)}, u32[]{:S(2)}) collective-permute-start(f32[128,256]{1,0:T(8,128)S(1)} %slice.53), channel_id=1, source_target_pairs={{0,4},{8,0},{16,8},{24,16},{28,24},{20,28},{12,20},{4,12},{1,5},{9... | collective-permute-start | bytes 393224 | tf_op jit(solution)/shard_map/ppermute | solution.py:253
  91.1 1.7 %shard_map.49.refs_6_ = f32[2048,256]{1,0:T(8,128)} custom-call(f32[64,512]{1,0:T(8,128)S(1)} %shard_map.43.refs_0_, f32[64,512]{1,0:T(8,128)S(1)} %shard_map.44.refs_1_, f32[64,512]{1,0:T(8,128)S(1)} %shard_map.45.refs_2_, f32[64,512]{1,0:T(8,128)S(1)} %shard_map.46.refs_3_, f32[256,256]{1,0:T(8,128)S(1)} %add_add_fusion.refs_4_, ...), custom_call_target="tpu_custom_call" | custom-call | flops 704643072 | bytes 2359296 | tf_op jit(solution)/shard_map/pallas_call | solution.py:42
  (59 shorter events, 14.2 us)
Async XLA Ops:
  4.9 1.6 %collective-permute-start = (f32[192,256]{1,0:T(8,128)S(1)}, f32[192,256]{1,0:T(8,128)S(1)}, u32[]{:S(2)}, u32[]{:S(2)}) collective-permute-start(f32[192,256]{1,0:T(8,128)S(1)} %get-tuple-element.17), channel_id=1, source_target_pairs={{0,1},{1,0},{2,3},{3,2},{4,5},{5,4},{6,7},{7,6},{8,9},{9,8},{10,11... | collective-permute-start | bytes 589832 | tf_op jit(solution)/shard_map/ppermute | solution.py:188
  6.6 8.1 %collective-permute-start.1 = (f32[192,256]{1,0:T(8,128)S(1)}, f32[192,256]{1,0:T(8,128)S(1)}, u32[]{:S(2)}, u32[]{:S(2)}) collective-permute-start(f32[192,256]{1,0:T(8,128)S(1)} %add.54), channel_id=1, source_target_pairs={{0,2},{1,3},{2,0},{3,1},{4,6},{5,7},{6,4},{7,5},{8,10},{9,11},{10,... | collective-permute-start | bytes 589832 | tf_op jit(solution)/shard_map/ppermute | solution.py:188
  14.7 1.5 %collective-permute-start.2 = (f32[192,256]{1,0:T(8,128)S(1)}, f32[192,256]{1,0:T(8,128)S(1)}, u32[]{:S(2)}, u32[]{:S(2)}) collective-permute-start(f32[192,256]{1,0:T(8,128)S(1)} %add.55.mine_ref.refs_0_), channel_id=1, source_target_pairs={{0,1},{1,0},{2,3},{3,2},{4,5},{5,4},{6,7},{7,6},{8,9},{9,8},{10,11... | collective-permute-start | bytes 589832 | tf_op jit(solution)/shard_map/ppermute | solution.py:188
  16.7 5.6 %collective-permute-start.7 = (f32[128,256]{1,0:T(8,128)S(1)}, f32[128,256]{1,0:T(8,128)S(1)}, u32[]{:S(2)}, u32[]{:S(2)}) collective-permute-start(f32[128,256]{1,0:T(8,128)S(1)} %get-tuple-element.31), channel_id=1, source_target_pairs={{0,8},{8,16},{16,24},{24,28},{28,20},{20,12},{12,4},{4,0},{1,9},{9... | collective-permute-start | bytes 393224 | tf_op jit(solution)/shard_map/ppermute | solution.py:253
  18.6 5.6 %collective-permute-start.11 = (f32[128,256]{1,0:T(8,128)S(1)}, f32[128,256]{1,0:T(8,128)S(1)}, u32[]{:S(2)}, u32[]{:S(2)}) collective-permute-start(f32[128,256]{1,0:T(8,128)S(1)} %get-tuple-element.30), channel_id=1, source_target_pairs={{0,4},{8,0},{16,8},{24,16},{28,24},{20,28},{12,20},{4,12},{1,5},{9... | collective-permute-start | bytes 393224 | tf_op jit(solution)/shard_map/ppermute | solution.py:253
  22.4 7.6 %collective-permute-start.8 = (f32[256,256]{1,0:T(8,128)S(1)}, f32[256,256]{1,0:T(8,128)S(1)}, u32[]{:S(2)}, u32[]{:S(2)}) collective-permute-start(f32[256,256]{1,0:T(8,128)S(1)} %pad_add_fusion.1), channel_id=1, source_target_pairs={{0,8},{8,16},{16,24},{24,28},{28,20},{20,12},{12,4},{4,0},{1,9},{9... | collective-permute-start | bytes 786440 | tf_op jit(solution)/shard_map/ppermute | solution.py:253
  24.3 7.6 %collective-permute-start.12 = (f32[256,256]{1,0:T(8,128)S(1)}, f32[256,256]{1,0:T(8,128)S(1)}, u32[]{:S(2)}, u32[]{:S(2)}) collective-permute-start(f32[256,256]{1,0:T(8,128)S(1)} %pad_add_fusion), channel_id=1, source_target_pairs={{0,4},{8,0},{16,8},{24,16},{28,24},{20,28},{12,20},{4,12},{1,5},{9... | collective-permute-start | bytes 786440 | tf_op jit(solution)/shard_map/ppermute | solution.py:253
  30.0 6.7 %collective-permute-start.9 = (f32[256,256]{1,0:T(8,128)S(1)}, f32[256,256]{1,0:T(8,128)S(1)}, u32[]{:S(2)}, u32[]{:S(2)}) collective-permute-start(f32[256,256]{1,0:T(8,128)S(1)} %add.60), channel_id=1, source_target_pairs={{0,8},{8,16},{16,24},{24,28},{28,20},{20,12},{12,4},{4,0},{1,9},{9... | collective-permute-start | bytes 786440 | tf_op jit(solution)/shard_map/ppermute | solution.py:253
  31.8 6.7 %collective-permute-start.13 = (f32[256,256]{1,0:T(8,128)S(1)}, f32[256,256]{1,0:T(8,128)S(1)}, u32[]{:S(2)}, u32[]{:S(2)}) collective-permute-start(f32[256,256]{1,0:T(8,128)S(1)} %add.63), channel_id=1, source_target_pairs={{0,4},{8,0},{16,8},{24,16},{28,24},{20,28},{12,20},{4,12},{1,5},{9... | collective-permute-start | bytes 786440 | tf_op jit(solution)/shard_map/ppermute | solution.py:253
  36.8 6.4 %collective-permute-start.10 = (f32[256,256]{1,0:T(8,128)S(1)}, f32[256,256]{1,0:T(8,128)S(1)}, u32[]{:S(2)}, u32[]{:S(2)}) collective-permute-start(f32[256,256]{1,0:T(8,128)S(1)} %add.61), channel_id=1, source_target_pairs={{0,8},{8,16},{16,24},{24,28},{28,20},{20,12},{12,4},{4,0},{1,9},{9... | collective-permute-start | bytes 786440 | tf_op jit(solution)/shard_map/ppermute | solution.py:253
  38.6 6.4 %collective-permute-start.14 = (f32[256,256]{1,0:T(8,128)S(1)}, f32[256,256]{1,0:T(8,128)S(1)}, u32[]{:S(2)}, u32[]{:S(2)}) collective-permute-start(f32[256,256]{1,0:T(8,128)S(1)} %add.64), channel_id=1, source_target_pairs={{0,4},{8,0},{16,8},{24,16},{28,24},{20,28},{12,20},{4,12},{1,5},{9... | collective-permute-start | bytes 786440 | tf_op jit(solution)/shard_map/ppermute | solution.py:253
  45.1 9.0 %collective-permute-start.15 = (f32[256,256]{1,0:T(8,128)S(1)}, f32[256,256]{1,0:T(8,128)S(1)}, u32[]{:S(2)}, u32[]{:S(2)}) collective-permute-start(f32[256,256]{1,0:T(8,128)S(1)} %add_add_fusion.refs_4_), channel_id=1, source_target_pairs={{0,8},{8,16},{16,24},{24,28},{28,20},{20,12},{12,4},{4,0},{1,9},{9... | collective-permute-start | bytes 786440 | tf_op jit(solution)/shard_map/ppermute | solution.py:253
  46.7 9.4 %collective-permute-start.19 = (f32[256,256]{1,0:T(8,128)S(1)}, f32[256,256]{1,0:T(8,128)S(1)}, u32[]{:S(2)}, u32[]{:S(2)}) collective-permute-start(f32[256,256]{1,0:T(8,128)S(1)} %add_add_fusion.refs_4_), channel_id=1, source_target_pairs={{0,4},{8,0},{16,8},{24,16},{28,24},{20,28},{12,20},{4,12},{1,5},{9... | collective-permute-start | bytes 786440 | tf_op jit(solution)/shard_map/ppermute | solution.py:253
  47.7 6.3 %collective-permute-start.3 = (f32[192,128]{1,0:T(8,128)S(1)}, f32[192,128]{1,0:T(8,128)S(1)}, u32[]{:S(2)}, u32[]{:S(2)}) collective-permute-start(f32[192,128]{1,0:T(8,128)S(1)} %shard_map.42), channel_id=1, source_target_pairs={{0,4},{4,0},{8,12},{12,8},{16,20},{20,16},{24,28},{28,24},{1,5},{5... | collective-permute-start | bytes 294920 | tf_op jit(solution)/shard_map/ppermute | solution.py:188
  54.0 5.7 %collective-permute-start.4 = (f32[192,128]{1,0:T(8,128)S(1)}, f32[192,128]{1,0:T(8,128)S(1)}, u32[]{:S(2)}, u32[]{:S(2)}) collective-permute-start(f32[192,128]{1,0:T(8,128)S(1)} %add.56), channel_id=1, source_target_pairs={{0,8},{4,12},{8,0},{12,4},{16,24},{20,28},{24,16},{28,20},{1,9},{5... | collective-permute-start | bytes 294920 | tf_op jit(solution)/shard_map/ppermute | solution.py:188
  54.1 15.2 %collective-permute-start.16 = (f32[256,256]{1,0:T(8,128)S(1)}, f32[256,256]{1,0:T(8,128)S(1)}, u32[]{:S(2)}, u32[]{:S(2)}) collective-permute-start(f32[256,256]{1,0:T(8,128)S(1)} %collective-permute-done.15.refs_5_), channel_id=1, source_target_pairs={{0,8},{8,16},{16,24},{24,28},{28,20},{20,12},{12,4},{4,0},{1,9},{9... | collective-permute-start | bytes 786440 | tf_op jit(solution)/shard_map/ppermute | solution.py:253
  56.1 13.2 %collective-permute-start.20 = (f32[256,256]{1,0:T(8,128)S(1)}, f32[256,256]{1,0:T(8,128)S(1)}, u32[]{:S(2)}, u32[]{:S(2)}) collective-permute-start(f32[256,256]{1,0:T(8,128)S(1)} %collective-permute-done.19.refs_6_), channel_id=1, source_target_pairs={{0,4},{8,0},{16,8},{24,16},{28,24},{20,28},{12,20},{4,12},{1,5},{9... | collective-permute-start | bytes 786440 | tf_op jit(solution)/shard_map/ppermute | solution.py:253
  59.7 9.4 %collective-permute-start.5 = (f32[192,128]{1,0:T(8,128)S(1)}, f32[192,128]{1,0:T(8,128)S(1)}, u32[]{:S(2)}, u32[]{:S(2)}) collective-permute-start(f32[192,128]{1,0:T(8,128)S(1)} %add.57), channel_id=1, source_target_pairs={{0,16},{4,20},{8,24},{12,28},{16,0},{20,4},{24,8},{28,12},{1,17},{... | collective-permute-start | bytes 294920 | tf_op jit(solution)/shard_map/ppermute | solution.py:188
  69.1 2.2 %collective-permute-start.6 = (f32[192,128]{1,0:T(8,128)S(1)}, f32[192,128]{1,0:T(8,128)S(1)}, u32[]{:S(2)}, u32[]{:S(2)}) collective-permute-start(f32[192,128]{1,0:T(8,128)S(1)} %add.58), channel_id=1, source_target_pairs={{0,1},{1,0},{2,3},{3,2},{4,5},{5,4},{6,7},{7,6},{8,9},{9,8},{10,11... | collective-permute-start | bytes 294920 | tf_op jit(solution)/shard_map/ppermute | solution.py:188
  69.2 18.9 %collective-permute-start.17 = (f32[256,256]{1,0:T(8,128)S(1)}, f32[256,256]{1,0:T(8,128)S(1)}, u32[]{:S(2)}, u32[]{:S(2)}) collective-permute-start(f32[256,256]{1,0:T(8,128)S(1)} %collective-permute-done.16.refs_7_), channel_id=1, source_target_pairs={{0,8},{8,16},{16,24},{24,28},{28,20},{20,12},{12,4},{4,0},{1,9},{9... | collective-permute-start | bytes 786440 | tf_op jit(solution)/shard_map/ppermute | solution.py:253
  69.3 19.2 %collective-permute-start.21 = (f32[256,256]{1,0:T(8,128)S(1)}, f32[256,256]{1,0:T(8,128)S(1)}, u32[]{:S(2)}, u32[]{:S(2)}) collective-permute-start(f32[256,256]{1,0:T(8,128)S(1)} %collective-permute-done.20.refs_8_), channel_id=1, source_target_pairs={{0,4},{8,0},{16,8},{24,16},{28,24},{20,28},{12,20},{4,12},{1,5},{9... | collective-permute-start | bytes 786440 | tf_op jit(solution)/shard_map/ppermute | solution.py:253
  88.2 5.3 %collective-permute-start.18 = (f32[128,256]{1,0:T(8,128)S(1)}, f32[128,256]{1,0:T(8,128)S(1)}, u32[]{:S(2)}, u32[]{:S(2)}) collective-permute-start(f32[128,256]{1,0:T(8,128)S(1)} %slice.52), channel_id=1, source_target_pairs={{0,8},{8,16},{16,24},{24,28},{28,20},{20,12},{12,4},{4,0},{1,9},{9... | collective-permute-start | bytes 393224 | tf_op jit(solution)/shard_map/ppermute | solution.py:253
  88.5 5.3 %collective-permute-start.22 = (f32[128,256]{1,0:T(8,128)S(1)}, f32[128,256]{1,0:T(8,128)S(1)}, u32[]{:S(2)}, u32[]{:S(2)}) collective-permute-start(f32[128,256]{1,0:T(8,128)S(1)} %slice.53), channel_id=1, source_target_pairs={{0,4},{8,0},{16,8},{24,16},{28,24},{20,28},{12,20},{4,12},{1,5},{9... | collective-permute-start | bytes 393224 | tf_op jit(solution)/shard_map/ppermute | solution.py:253
where the time goes:
time: 95.2 us; the launch traced here: 95.1 us
  waiting for transfers between devices  41 us (43%)
  Pallas kernels  26.5 us (28%)
  starting transfers between devices  25.3 us (27%)
  other arithmetic  1.19 us (1%)
  between operations  1.08 us (1%)
    pallas_call x10, Pallas kernels, call(): pl.pallas_call(kernel, out_shape=outs, in_specs=specs or [VMEM] * len(arg...  26.5 us
    ppermute x7, waiting for transfers between devices, swap(): lax.ppermute(value, axis, [(i, i ^ mask) for i in range(lax.axis_size(axi...  22.1 us
    ppermute x16, waiting for transfers between devices, send(): return lax.ppermute(value, self.axis, pairs)  18.9 us
    ppermute x16, starting transfers between devices, send(): return lax.ppermute(value, self.axis, pairs)  17.2 us
    ppermute x7, starting transfers between devices, swap(): lax.ppermute(value, axis, [(i, i ^ mask) for i in range(lax.axis_size(axi...  8.11 us
  transfers between devices with their start and end apart: 23, of which 13 were waited for; matrix products, arithmetic and copies ran while one was open for 1% of the time, Pallas kernels for 22%

commit v1 on v0

--- a/solution.py
+++ b/solution.py
@@ -13,6 +13,7 @@
 ANY = pl.BlockSpec(memory_space=pltpu.HBM)
 F32, BF16 = jnp.float32, jnp.bfloat16
 MIB = 1 << 20
+PANEL = 32
 
 
 def mm(left, right, dims, precision=high):
@@ -58,30 +59,35 @@
 def factor_kernel(block, top, gram_ref, *refs):
     *above, out_ref, part = refs
     panel, n = out_ref.shape[0], gram_ref.shape[0]
+    lanes, group = 128, 8
     row = lax.broadcasted_iota(jnp.int32, (panel, n), 0)
     col = lax.broadcasted_iota(jnp.int32, (panel, n), 1)
-    sub = lax.broadcasted_iota(jnp.int32, (block, 2 * n), 0)
-    lanes = min(n, 128)
+    low = top // lanes * lanes
+    high_ = n + pl.cdiv(top + panel, lanes) * lanes
+    width = high_ - low
+    sub = lax.broadcasted_iota(jnp.int32, (group, width), 0)
 
     def wide(v):
-        return jnp.concatenate([v] * (2 * n // lanes), axis=1)
+        return jnp.concatenate([v] * (width // lanes), axis=1)
 
     eye = jnp.where(row + top == col, 1.0, 0.0).astype(F32)
-    rest = jnp.concatenate([gram_ref[top : top + panel, :], eye], axis=1)
+    rest = jnp.concatenate([gram_ref[top : top + panel, :], eye], axis=1)[:, low:high_]
     for ref in above:
-        rest = rest - mm(ref[:, top : top + panel], ref[...], ((0,), (0,)))
-    part[...] = rest
+        rest = rest - mm(ref[:, top : top + panel], ref[:, low:high_], ((0,), (0,)))
+    part[:, low:high_] = rest
+    if low > 0:
+        out_ref[:, :low] = jnp.zeros((panel, low), F32)
+    if high_ < 2 * n:
+        out_ref[:, high_:] = jnp.zeros((panel, 2 * n - high_), F32)
     for inner in range(0, panel, block):
-        k = top + inner
-        rows = part[inner : inner + block, :]
-        columns = [
-            jnp.broadcast_to(rows[:, k + j : k + j + 1], (block, lanes)) for j in range(block)
-        ]
-        d = {
-            (i, j): jnp.broadcast_to(columns[j][i : i + 1, :], (block, lanes))
-            for i in range(block)
-            for j in range(i, block)
-        }
+        k = top + inner - low
+        d, rows = {}, []
+        for g in range(0, block, group):
+            rows.append(part[inner + g : inner + g + group, low:high_])
+            for j in range(g, block):
+                c = jnp.broadcast_to(rows[-1][:, k + j : k + j + 1], (group, lanes))
+                for i in range(g, min(g + group, j + 1)):
+                    d[i, j] = jnp.broadcast_to(c[i - g : i - g + 1, :], (group, lanes))
         scale = []
         for i in range(block):
             scale.append(lax.rsqrt(d[i, i]))
@@ -90,32 +96,36 @@
             for j in range(i + 1, block):
                 for l in range(j, block):
                     d[j, l] = d[j, l] - d[i, j] * d[i, l]
-        done, solved = [], jnp.zeros((block, 2 * n), F32)
+        done, solved = [], []
         for i in range(block):
-            line = jnp.broadcast_to(rows[i : i + 1, :], (block, 2 * n))
+            g, at = divmod(i, group)
+            if at == 0:
+                solved.append(jnp.zeros((group, width), F32))
+            line = jnp.broadcast_to(rows[g][at : at + 1, :], (group, width))
             for m in range(i):
                 line = line - wide(d[m, i]) * done[m]
             line = line * wide(scale[i])
             done.append(line)
-            solved = jnp.where(sub == i, line, solved)
-        out_ref[inner : inner + block, :] = solved
+            solved[g] = jnp.where(sub == at, line, solved[g])
+        solved = jnp.concatenate(solved)
+        out_ref[inner : inner + block, low:high_] = solved
         if inner + block < panel:
-            part[inner + block :, :] -= mm(
-                solved[:, k + block : top + panel], solved, ((0,), (0,))
+            part[inner + block :, low:high_] -= mm(
+                solved[:, k + block : top + panel - low], solved, ((0,), (0,))
             )
 
 
 def factor_rows(gram, above):
     n = gram.shape[0]
-    panel = min(n, 64)
+    panel = min(n, PANEL)
     top = panel * len(above)
     (rows,) = call(
-        functools.partial(factor_kernel, 8, top),
+        functools.partial(factor_kernel, 16, top),
         [array((panel, 2 * n))],
         gram,
         *above,
         scratch=[pltpu.VMEM((panel, 2 * n), F32)],
-        flops=12 * n**3 // 4,
+        flops=12 * n * n * panel,
     )
     return rows
 
@@ -166,7 +176,7 @@
 def sketch_parts(snapshot, test_matrix, axis):
     points, depth = snapshot.shape
     width = test_matrix.shape[1]
-    chunks = 4
+    chunks = 8
     half = array((points // 2, width))
     return call(
         functools.partial(sketch_kernel, axis),
@@ -371,7 +381,7 @@
         left = ring.send(parts[-d] + left, -1)
     own = parts[0] + (right + left)
     panels = []
-    while len(panels) * 64 < gram.shape[0]:
+    while len(panels) * PANEL < gram.shape[0]:
         panels.append(factor_rows(gram, panels))
     early, late = {(0, 0): own}, {}
     right = left = own
@@ -393,7 +403,7 @@
     sketch = lax.psum(mm(snapshot, test_matrix, ((1,), (0,))), "cols")
     gram = lax.psum(mm(sketch, sketch, ((0,), (0,))), "rows")
     panels = []
-    while len(panels) * 64 < gram.shape[0]:
+    while len(panels) * PANEL < gram.shape[0]:
         panels.append(factor_rows(gram, panels))
     product = lax.psum(mm(snapshot, sketch, ((0,), (0,))), "rows")
     total = snapshot.shape[0] * lax.axis_size("rows")

time: 95.2 us -> 85.6 us (0.90)
  waiting for transfers between devices: 41 us -> 34.8 us
  Pallas kernels: 26.5 us -> 22.9 us
    ppermute x7, waiting for transfers between devices: 22.1 us -> 18.1 us  [swap(): lax.ppermute(value, axis, [(i, i ^ mask) for i in range(lax.axis_size(axi...]
    pallas_call x10 -> x14, Pallas kernels: 26.5 us -> 22.9 us  [call(): pl.pallas_call(kernel, out_shape=outs, in_specs=specs or [VMEM] * len(arg...]
    ppermute x16, waiting for transfers between devices: 18.9 us -> 16.7 us  [send(): return lax.ppermute(value, self.axis, pairs)]
  transfers between devices with their start and end apart: 23 -> 23, of which waited for: 13 -> 16; matrix products, arithmetic and copies ran while one was open for 1% -> 1% of each run, Pallas kernels for 22% -> 20%
where the time goes in v1:
time: 85.6 us; the launch traced here: 85.4 us
  waiting for transfers between devices  34.8 us (41%)
  starting transfers between devices  25.4 us (30%)
  Pallas kernels  22.9 us (27%)
  other arithmetic  1.18 us (1%)
  between operations  1.03 us (1%)
    pallas_call x14, Pallas kernels, call(): pl.pallas_call(kernel, out_shape=outs, in_specs=specs or [VMEM] * len(arg...  22.9 us
    ppermute x7, waiting for transfers between devices, swap(): lax.ppermute(value, axis, [(i, i ^ mask) for i in range(lax.axis_size(axi...  18.1 us
    ppermute x16, starting transfers between devices, send(): return lax.ppermute(value, self.axis, pairs)  17.8 us
    ppermute x16, waiting for transfers between devices, send(): return lax.ppermute(value, self.axis, pairs)  16.7 us
    ppermute x7, starting transfers between devices, swap(): lax.ppermute(value, axis, [(i, i ^ mask) for i in range(lax.axis_size(axi...  7.62 us
  transfers between devices with their start and end apart: 23, of which 16 were waited for; matrix products, arithmetic and copies ran while one was open for 1% of the time, Pallas kernels for 20%

profile of v1, /device:TPU:0, one launch (start us, length us, event | category | flops | bytes accessed | tf_op | source)
XLA Modules:
  0.0 85.4 jit_solution(10518921538667264403)
XLA Ops:
  0.6 4.3 %shard_map.41 = (f32[192,256]{1,0:T(8,128)S(1)}, f32[192,256]{1,0:T(8,128)S(1)}, bf16[384,2048]{1,0:T(8,128)(2,1)S(1)}, bf16[384,2048]{1,0:T(8,128)(2,1)S(1)}) custom-call(f32[384,2048]{1,0:T(8,128)} %snap_any.1, f32[2048,256]{1,0:T(8,128)} %test_any.1), custom_call_target="tpu_custom_call" | custom-call | flops 1207959552 | bytes 5242880 | tf_op jit(solution)/shard_map/pallas_call | solution.py:43
  6.6 2.9 %collective-permute-start.1 = (f32[192,256]{1,0:T(8,128)S(1)}, f32[192,256]{1,0:T(8,128)S(1)}, u32[]{:S(2)}, u32[]{:S(2)}) collective-permute-start(f32[192,256]{1,0:T(8,128)S(1)} %add.54), channel_id=1, source_target_pairs={{0,2},{1,3},{2,0},{3,1},{4,6},{5,7},{6,4},{7,5},{8,10},{9,11},{10,... | collective-permute-start | bytes 589832 | tf_op jit(solution)/shard_map/ppermute | solution.py:198
  9.5 5.2 %collective-permute-done.1 = f32[192,256]{1,0:T(8,128)S(1)} collective-permute-done((f32[192,256]{1,0:T(8,128)S(1)}, f32[192,256]{1,0:T(8,128)S(1)}, u32[]{:S(2)}, u32[]{:S(2)}) %collective-permute-start.1) | collective-permute-done | bytes 196640 | tf_op jit(solution)/shard_map/ppermute | solution.py:198
  16.8 1.9 %collective-permute-start.7 = (f32[128,256]{1,0:T(8,128)S(1)}, f32[128,256]{1,0:T(8,128)S(1)}, u32[]{:S(2)}, u32[]{:S(2)}) collective-permute-start(f32[128,256]{1,0:T(8,128)S(1)} %get-tuple-element.31), channel_id=1, source_target_pairs={{0,8},{8,16},{16,24},{24,28},{28,20},{20,12},{12,4},{4,0},{1,9},{9... | collective-permute-start | bytes 393224 | tf_op jit(solution)/shard_map/ppermute | solution.py:263
  19.5 1.8 %collective-permute-start.11 = (f32[128,256]{1,0:T(8,128)S(1)}, f32[128,256]{1,0:T(8,128)S(1)}, u32[]{:S(2)}, u32[]{:S(2)}) collective-permute-start(f32[128,256]{1,0:T(8,128)S(1)} %get-tuple-element.30), channel_id=1, source_target_pairs={{0,4},{8,0},{16,8},{24,16},{28,24},{20,28},{12,20},{4,12},{1,5},{9... | collective-permute-start | bytes 393224 | tf_op jit(solution)/shard_map/ppermute | solution.py:263
  21.3 1.7 %shard_map.52 = (f32[256,256]{1,0:T(8,128)S(1)}, f32[256,256]{1,0:T(8,128)S(1)}, f32[256,256]{1,0:T(8,128)S(1)}, f32[256,256]{1,0:T(8,128)S(1)}, f32[256,256]{1,...) custom-call(bf16[384,256]{1,0:T(8,128)(2,1)S(1)} %get-tuple-element.20.refs_0_, ...), custom_call_target="tpu_custom_call" | custom-call | flops 1056964608 | bytes 3538944 | tf_op jit(solution)/shard_map/pallas_call | solution.py:43
  23.0 1.5 %collective-permute-done.3 = f32[192,128]{1,0:T(8,128)S(1)} collective-permute-done((f32[192,128]{1,0:T(8,128)S(1)}, f32[192,128]{1,0:T(8,128)S(1)}, u32[]{:S(2)}, u32[]{:S(2)}) %collective-permute-start.3) | collective-permute-done | bytes 98336 | tf_op jit(solution)/shard_map/ppermute | solution.py:198
  27.7 2.3 %collective-permute-done.4 = f32[192,128]{1,0:T(8,128)S(1)} collective-permute-done((f32[192,128]{1,0:T(8,128)S(1)}, f32[192,128]{1,0:T(8,128)S(1)}, u32[]{:S(2)}, u32[]{:S(2)}) %collective-permute-start.4) | collective-permute-done | bytes 98336 | tf_op jit(solution)/shard_map/ppermute | solution.py:198
  30.1 2.7 %collective-permute-start.5 = (f32[192,128]{1,0:T(8,128)S(1)}, f32[192,128]{1,0:T(8,128)S(1)}, u32[]{:S(2)}, u32[]{:S(2)}) collective-permute-start(f32[192,128]{1,0:T(8,128)S(1)} %add.57), channel_id=1, source_target_pairs={{0,16},{4,20},{8,24},{12,28},{16,0},{20,4},{24,8},{28,12},{1,17},{... | collective-permute-start | bytes 294920 | tf_op jit(solution)/shard_map/ppermute | solution.py:198
  32.8 6.5 %collective-permute-done.5 = f32[192,128]{1,0:T(8,128)S(1)} collective-permute-done((f32[192,128]{1,0:T(8,128)S(1)}, f32[192,128]{1,0:T(8,128)S(1)}, u32[]{:S(2)}, u32[]{:S(2)}) %collective-permute-start.5) | collective-permute-done | bytes 98336 | tf_op jit(solution)/shard_map/ppermute | solution.py:198
  39.8 1.8 %collective-permute-start.13 = (f32[256,256]{1,0:T(8,128)S(1)}, f32[256,256]{1,0:T(8,128)S(1)}, u32[]{:S(2)}, u32[]{:S(2)}) collective-permute-start(f32[256,256]{1,0:T(8,128)S(1)} %add.63), channel_id=1, source_target_pairs={{0,4},{8,0},{16,8},{24,16},{28,24},{20,28},{12,20},{4,12},{1,5},{9... | collective-permute-start | bytes 786440 | tf_op jit(solution)/shard_map/ppermute | solution.py:263
  42.9 5.3 %collective-permute-done.9 = f32[256,256]{1,0:T(8,128)S(1)} collective-permute-done((f32[256,256]{1,0:T(8,128)S(1)}, f32[256,256]{1,0:T(8,128)S(1)}, u32[]{:S(2)}, u32[]{:S(2)}) %collective-permute-start.9) | collective-permute-done | bytes 262176 | tf_op jit(solution)/shard_map/ppermute | solution.py:263
  48.6 1.8 %collective-permute-start.14 = (f32[256,256]{1,0:T(8,128)S(1)}, f32[256,256]{1,0:T(8,128)S(1)}, u32[]{:S(2)}, u32[]{:S(2)}) collective-permute-start(f32[256,256]{1,0:T(8,128)S(1)} %add.64), channel_id=1, source_target_pairs={{0,4},{8,0},{16,8},{24,16},{28,24},{20,28},{12,20},{4,12},{1,5},{9... | collective-permute-start | bytes 786440 | tf_op jit(solution)/shard_map/ppermute | solution.py:263
  50.4 1.6 %shard_map.44.refs_1_ = f32[32,512]{1,0:T(8,128)S(1)} custom-call(f32[256,256]{1,0:T(8,128)S(1)} %select_maximum_fusion.gram_ref, f32[32,512]{1,0:T(8,128)S(1)} %shard_map.43.refs_0_), custom_call_target="tpu_custom_call" | custom-call | flops 25165824 | bytes 327680 | tf_op jit(solution)/shard_map/pallas_call | solution.py:43
  52.0 1.6 %shard_map.45.refs_2_ = f32[32,512]{1,0:T(8,128)S(1)} custom-call(f32[256,256]{1,0:T(8,128)S(1)} %select_maximum_fusion.gram_ref, f32[32,512]{1,0:T(8,128)S(1)} %shard_map.43.refs_0_, f32[32,512]{1,0:T(8,128)S(1)} %shard_map.44.refs_1_), custom_call_target="tpu_custom_call" | custom-call | flops 25165824 | bytes 393216 | tf_op jit(solution)/shard_map/pallas_call | solution.py:43
  53.6 2.5 %collective-permute-done.10 = f32[256,256]{1,0:T(8,128)S(1)} collective-permute-done((f32[256,256]{1,0:T(8,128)S(1)}, f32[256,256]{1,0:T(8,128)S(1)}, u32[]{:S(2)}, u32[]{:S(2)}) %collective-permute-start.10) | collective-permute-done | bytes 262176 | tf_op jit(solution)/shard_map/ppermute | solution.py:263
  58.4 1.7 %shard_map.46.refs_3_ = f32[32,512]{1,0:T(8,128)S(1)} custom-call(f32[256,256]{1,0:T(8,128)S(1)} %select_maximum_fusion.gram_ref, f32[32,512]{1,0:T(8,128)S(1)} %shard_map.43.refs_0_, f32[32,512]{1,0:T(8,128)S(1)} %shard_map.44.refs_1_, f32[32,512]{1,0:T(8,128)S(1)} %shard_map.45.refs_2_), custom_call_target="tpu_custom_call" | custom-call | flops 25165824 | bytes 458752 | tf_op jit(solution)/shard_map/pallas_call | solution.py:43
  60.1 1.6 %shard_map.47.refs_4_ = f32[32,512]{1,0:T(8,128)S(1)} custom-call(f32[256,256]{1,0:T(8,128)S(1)} %select_maximum_fusion.gram_ref, f32[32,512]{1,0:T(8,128)S(1)} %shard_map.43.refs_0_, f32[32,512]{1,0:T(8,128)S(1)} %shard_map.44.refs_1_, f32[32,512]{1,0:T(8,128)S(1)} %shard_map.45.refs_2_, f32[32,512]{1,0:T(8,128)S(1)} %shard_map.46.refs_3_), custom_call_target="tpu_custom_call" | custom-call | flops 25165824 | bytes 524288 | tf_op jit(solution)/shard_map/pallas_call | solution.py:43
  65.3 1.8 %shard_map.48.refs_5_ = f32[32,512]{1,0:T(8,128)S(1)} custom-call(f32[256,256]{1,0:T(8,128)S(1)} %select_maximum_fusion.gram_ref, f32[32,512]{1,0:T(8,128)S(1)} %shard_map.43.refs_0_, f32[32,512]{1,0:T(8,128)S(1)} %shard_map.44.refs_1_, f32[32,512]{1,0:T(8,128)S(1)} %shard_map.45.refs_2_, f32[32,512]{1,0:T(8,128)S(1)} %shard_map.46.refs_3_, ...), custom_call_target="tpu_custom_call" | custom-call | flops 25165824 | bytes 589824 | tf_op jit(solution)/shard_map/pallas_call | solution.py:43
  67.0 1.8 %shard_map.49.refs_6_ = f32[32,512]{1,0:T(8,128)S(1)} custom-call(f32[256,256]{1,0:T(8,128)S(1)} %select_maximum_fusion.gram_ref, f32[32,512]{1,0:T(8,128)S(1)} %shard_map.43.refs_0_, f32[32,512]{1,0:T(8,128)S(1)} %shard_map.44.refs_1_, f32[32,512]{1,0:T(8,128)S(1)} %shard_map.45.refs_2_, f32[32,512]{1,0:T(8,128)S(1)} %shard_map.46.refs_3_, ...), custom_call_target="tpu_custom_call" | custom-call | flops 25165824 | bytes 655360 | tf_op jit(solution)/shard_map/pallas_call | solution.py:43
  68.8 1.5 %collective-permute-done.16.refs_11_ = f32[256,256]{1,0:T(8,128)S(1)} collective-permute-done((f32[256,256]{1,0:T(8,128)S(1)}, f32[256,256]{1,0:T(8,128)S(1)}, u32[]{:S(2)}, u32[]{:S(2)}) %collective-permute-start.16) | collective-permute-done | bytes 262176 | tf_op jit(solution)/shard_map/ppermute | solution.py:263
  72.4 1.9 %shard_map.50.refs_7_ = f32[32,512]{1,0:T(8,128)S(1)} custom-call(f32[256,256]{1,0:T(8,128)S(1)} %select_maximum_fusion.gram_ref, f32[32,512]{1,0:T(8,128)S(1)} %shard_map.43.refs_0_, f32[32,512]{1,0:T(8,128)S(1)} %shard_map.44.refs_1_, f32[32,512]{1,0:T(8,128)S(1)} %shard_map.45.refs_2_, f32[32,512]{1,0:T(8,128)S(1)} %shard_map.46.refs_3_, ...), custom_call_target="tpu_custom_call" | custom-call | flops 25165824 | bytes 720896 | tf_op jit(solution)/shard_map/pallas_call | solution.py:43
  74.3 3.8 %collective-permute-done.17.refs_13_ = f32[256,256]{1,0:T(8,128)S(1)} collective-permute-done((f32[256,256]{1,0:T(8,128)S(1)}, f32[256,256]{1,0:T(8,128)S(1)}, u32[]{:S(2)}, u32[]{:S(2)}) %collective-permute-start.17) | collective-permute-done | bytes 262176 | tf_op jit(solution)/shard_map/ppermute | solution.py:263
  81.1 1.7 %shard_map.53.refs_10_ = f32[2048,256]{1,0:T(8,128)} custom-call(f32[32,512]{1,0:T(8,128)S(1)} %shard_map.43.refs_0_, f32[32,512]{1,0:T(8,128)S(1)} %shard_map.44.refs_1_, f32[32,512]{1,0:T(8,128)S(1)} %shard_map.45.refs_2_, f32[32,512]{1,0:T(8,128)S(1)} %shard_map.46.refs_3_, f32[32,512]{1,0:T(8,128)S(1)} %shard_map.47.refs_4_, ...), custom_call_target="tpu_custom_call" | custom-call | flops 704643072 | bytes 2359296 | tf_op jit(solution)/shard_map/pallas_call | solution.py:43
  (67 shorter events, 23.0 us)
Async XLA Ops:
  5.0 1.6 %collective-permute-start = (f32[192,256]{1,0:T(8,128)S(1)}, f32[192,256]{1,0:T(8,128)S(1)}, u32[]{:S(2)}, u32[]{:S(2)}) collective-permute-start(f32[192,256]{1,0:T(8,128)S(1)} %get-tuple-element.17), channel_id=1, source_target_pairs={{0,1},{1,0},{2,3},{3,2},{4,5},{5,4},{6,7},{7,6},{8,9},{9,8},{10,11... | collective-permute-start | bytes 589832 | tf_op jit(solution)/shard_map/ppermute | solution.py:198
  6.6 8.1 %collective-permute-start.1 = (f32[192,256]{1,0:T(8,128)S(1)}, f32[192,256]{1,0:T(8,128)S(1)}, u32[]{:S(2)}, u32[]{:S(2)}) collective-permute-start(f32[192,256]{1,0:T(8,128)S(1)} %add.54), channel_id=1, source_target_pairs={{0,2},{1,3},{2,0},{3,1},{4,6},{5,7},{6,4},{7,5},{8,10},{9,11},{10,... | collective-permute-start | bytes 589832 | tf_op jit(solution)/shard_map/ppermute | solution.py:198
  14.8 1.5 %collective-permute-start.2 = (f32[192,256]{1,0:T(8,128)S(1)}, f32[192,256]{1,0:T(8,128)S(1)}, u32[]{:S(2)}, u32[]{:S(2)}) collective-permute-start(f32[192,256]{1,0:T(8,128)S(1)} %add.55.mine_ref.refs_0_), channel_id=1, source_target_pairs={{0,1},{1,0},{2,3},{3,2},{4,5},{5,4},{6,7},{7,6},{8,9},{9,8},{10,11... | collective-permute-start | bytes 589832 | tf_op jit(solution)/shard_map/ppermute | solution.py:198
  16.8 8.8 %collective-permute-start.7 = (f32[128,256]{1,0:T(8,128)S(1)}, f32[128,256]{1,0:T(8,128)S(1)}, u32[]{:S(2)}, u32[]{:S(2)}) collective-permute-start(f32[128,256]{1,0:T(8,128)S(1)} %get-tuple-element.31), channel_id=1, source_target_pairs={{0,8},{8,16},{16,24},{24,28},{28,20},{20,12},{12,4},{4,0},{1,9},{9... | collective-permute-start | bytes 393224 | tf_op jit(solution)/shard_map/ppermute | solution.py:263
  19.2 5.3 %collective-permute-start.3 = (f32[192,128]{1,0:T(8,128)S(1)}, f32[192,128]{1,0:T(8,128)S(1)}, u32[]{:S(2)}, u32[]{:S(2)}) collective-permute-start(f32[192,128]{1,0:T(8,128)S(1)} %shard_map.42), channel_id=1, source_target_pairs={{0,4},{4,0},{8,12},{12,8},{16,20},{20,16},{24,28},{28,24},{1,5},{5... | collective-permute-start | bytes 294920 | tf_op jit(solution)/shard_map/ppermute | solution.py:198
  19.5 7.2 %collective-permute-start.11 = (f32[128,256]{1,0:T(8,128)S(1)}, f32[128,256]{1,0:T(8,128)S(1)}, u32[]{:S(2)}, u32[]{:S(2)}) collective-permute-start(f32[128,256]{1,0:T(8,128)S(1)} %get-tuple-element.30), channel_id=1, source_target_pairs={{0,4},{8,0},{16,8},{24,16},{28,24},{20,28},{12,20},{4,12},{1,5},{9... | collective-permute-start | bytes 393224 | tf_op jit(solution)/shard_map/ppermute | solution.py:263
  24.5 5.6 %collective-permute-start.4 = (f32[192,128]{1,0:T(8,128)S(1)}, f32[192,128]{1,0:T(8,128)S(1)}, u32[]{:S(2)}, u32[]{:S(2)}) collective-permute-start(f32[192,128]{1,0:T(8,128)S(1)} %add.56), channel_id=1, source_target_pairs={{0,8},{4,12},{8,0},{12,4},{16,24},{20,28},{24,16},{28,20},{1,9},{5... | collective-permute-start | bytes 294920 | tf_op jit(solution)/shard_map/ppermute | solution.py:198
  25.6 13.8 %collective-permute-start.8 = (f32[256,256]{1,0:T(8,128)S(1)}, f32[256,256]{1,0:T(8,128)S(1)}, u32[]{:S(2)}, u32[]{:S(2)}) collective-permute-start(f32[256,256]{1,0:T(8,128)S(1)} %pad_add_fusion.1), channel_id=1, source_target_pairs={{0,8},{8,16},{16,24},{24,28},{28,20},{20,12},{12,4},{4,0},{1,9},{9... | collective-permute-start | bytes 786440 | tf_op jit(solution)/shard_map/ppermute | solution.py:263
  26.7 13.0 %collective-permute-start.12 = (f32[256,256]{1,0:T(8,128)S(1)}, f32[256,256]{1,0:T(8,128)S(1)}, u32[]{:S(2)}, u32[]{:S(2)}) collective-permute-start(f32[256,256]{1,0:T(8,128)S(1)} %pad_add_fusion), channel_id=1, source_target_pairs={{0,4},{8,0},{16,8},{24,16},{28,24},{20,28},{12,20},{4,12},{1,5},{9... | collective-permute-start | bytes 786440 | tf_op jit(solution)/shard_map/ppermute | solution.py:263
  30.1 9.2 %collective-permute-start.5 = (f32[192,128]{1,0:T(8,128)S(1)}, f32[192,128]{1,0:T(8,128)S(1)}, u32[]{:S(2)}, u32[]{:S(2)}) collective-permute-start(f32[192,128]{1,0:T(8,128)S(1)} %add.57), channel_id=1, source_target_pairs={{0,16},{4,20},{8,24},{12,28},{16,0},{20,4},{24,8},{28,12},{1,17},{... | collective-permute-start | bytes 294920 | tf_op jit(solution)/shard_map/ppermute | solution.py:198
  39.3 2.3 %collective-permute-start.6 = (f32[192,128]{1,0:T(8,128)S(1)}, f32[192,128]{1,0:T(8,128)S(1)}, u32[]{:S(2)}, u32[]{:S(2)}) collective-permute-start(f32[192,128]{1,0:T(8,128)S(1)} %add.58), channel_id=1, source_target_pairs={{0,1},{1,0},{2,3},{3,2},{4,5},{5,4},{6,7},{7,6},{8,9},{9,8},{10,11... | collective-permute-start | bytes 294920 | tf_op jit(solution)/shard_map/ppermute | solution.py:198
  39.5 8.7 %collective-permute-start.9 = (f32[256,256]{1,0:T(8,128)S(1)}, f32[256,256]{1,0:T(8,128)S(1)}, u32[]{:S(2)}, u32[]{:S(2)}) collective-permute-start(f32[256,256]{1,0:T(8,128)S(1)} %add.60), channel_id=1, source_target_pairs={{0,8},{8,16},{16,24},{24,28},{28,20},{20,12},{12,4},{4,0},{1,9},{9... | collective-permute-start | bytes 786440 | tf_op jit(solution)/shard_map/ppermute | solution.py:263
  39.8 8.8 %collective-permute-start.13 = (f32[256,256]{1,0:T(8,128)S(1)}, f32[256,256]{1,0:T(8,128)S(1)}, u32[]{:S(2)}, u32[]{:S(2)}) collective-permute-start(f32[256,256]{1,0:T(8,128)S(1)} %add.63), channel_id=1, source_target_pairs={{0,4},{8,0},{16,8},{24,16},{28,24},{20,28},{12,20},{4,12},{1,5},{9... | collective-permute-start | bytes 786440 | tf_op jit(solution)/shard_map/ppermute | solution.py:263
  48.2 7.9 %collective-permute-start.10 = (f32[256,256]{1,0:T(8,128)S(1)}, f32[256,256]{1,0:T(8,128)S(1)}, u32[]{:S(2)}, u32[]{:S(2)}) collective-permute-start(f32[256,256]{1,0:T(8,128)S(1)} %add.61), channel_id=1, source_target_pairs={{0,8},{8,16},{16,24},{24,28},{28,20},{20,12},{12,4},{4,0},{1,9},{9... | collective-permute-start | bytes 786440 | tf_op jit(solution)/shard_map/ppermute | solution.py:263
  48.6 7.7 %collective-permute-start.14 = (f32[256,256]{1,0:T(8,128)S(1)}, f32[256,256]{1,0:T(8,128)S(1)}, u32[]{:S(2)}, u32[]{:S(2)}) collective-permute-start(f32[256,256]{1,0:T(8,128)S(1)} %add.64), channel_id=1, source_target_pairs={{0,4},{8,0},{16,8},{24,16},{28,24},{20,28},{12,20},{4,12},{1,5},{9... | collective-permute-start | bytes 786440 | tf_op jit(solution)/shard_map/ppermute | solution.py:263
  56.3 6.9 %collective-permute-start.15 = (f32[256,256]{1,0:T(8,128)S(1)}, f32[256,256]{1,0:T(8,128)S(1)}, u32[]{:S(2)}, u32[]{:S(2)}) collective-permute-start(f32[256,256]{1,0:T(8,128)S(1)} %add_add_fusion.refs_8_), channel_id=1, source_target_pairs={{0,8},{8,16},{16,24},{24,28},{28,20},{20,12},{12,4},{4,0},{1,9},{9... | collective-permute-start | bytes 786440 | tf_op jit(solution)/shard_map/ppermute | solution.py:263
  57.4 7.3 %collective-permute-start.19 = (f32[256,256]{1,0:T(8,128)S(1)}, f32[256,256]{1,0:T(8,128)S(1)}, u32[]{:S(2)}, u32[]{:S(2)}) collective-permute-start(f32[256,256]{1,0:T(8,128)S(1)} %add_add_fusion.refs_8_), channel_id=1, source_target_pairs={{0,4},{8,0},{16,8},{24,16},{28,24},{20,28},{12,20},{4,12},{1,5},{9... | collective-permute-start | bytes 786440 | tf_op jit(solution)/shard_map/ppermute | solution.py:263
  63.2 7.1 %collective-permute-start.16 = (f32[256,256]{1,0:T(8,128)S(1)}, f32[256,256]{1,0:T(8,128)S(1)}, u32[]{:S(2)}, u32[]{:S(2)}) collective-permute-start(f32[256,256]{1,0:T(8,128)S(1)} %collective-permute-done.15.refs_9_), channel_id=1, source_target_pairs={{0,8},{8,16},{16,24},{24,28},{28,20},{20,12},{12,4},{4,0},{1,9},{9... | collective-permute-start | bytes 786440 | tf_op jit(solution)/shard_map/ppermute | solution.py:263
  64.6 6.7 %collective-permute-start.20 = (f32[256,256]{1,0:T(8,128)S(1)}, f32[256,256]{1,0:T(8,128)S(1)}, u32[]{:S(2)}, u32[]{:S(2)}) collective-permute-start(f32[256,256]{1,0:T(8,128)S(1)} %collective-permute-done.19.refs_10_), channel_id=1, source_target_pairs={{0,4},{8,0},{16,8},{24,16},{28,24},{20,28},{12,20},{4,12},{1,5},{9... | collective-permute-start | bytes 786440 | tf_op jit(solution)/shard_map/ppermute | solution.py:263
  70.4 7.8 %collective-permute-start.17 = (f32[256,256]{1,0:T(8,128)S(1)}, f32[256,256]{1,0:T(8,128)S(1)}, u32[]{:S(2)}, u32[]{:S(2)}) collective-permute-start(f32[256,256]{1,0:T(8,128)S(1)} %collective-permute-done.16.refs_11_), channel_id=1, source_target_pairs={{0,8},{8,16},{16,24},{24,28},{28,20},{20,12},{12,4},{4,0},{1,9},{9... | collective-permute-start | bytes 786440 | tf_op jit(solution)/shard_map/ppermute | solution.py:263
  71.3 7.8 %collective-permute-start.21 = (f32[256,256]{1,0:T(8,128)S(1)}, f32[256,256]{1,0:T(8,128)S(1)}, u32[]{:S(2)}, u32[]{:S(2)}) collective-permute-start(f32[256,256]{1,0:T(8,128)S(1)} %collective-permute-done.20.refs_12_), channel_id=1, source_target_pairs={{0,4},{8,0},{16,8},{24,16},{28,24},{20,28},{12,20},{4,12},{1,5},{9... | collective-permute-start | bytes 786440 | tf_op jit(solution)/shard_map/ppermute | solution.py:263
  78.2 5.0 %collective-permute-start.18 = (f32[128,256]{1,0:T(8,128)S(1)}, f32[128,256]{1,0:T(8,128)S(1)}, u32[]{:S(2)}, u32[]{:S(2)}) collective-permute-start(f32[128,256]{1,0:T(8,128)S(1)} %slice.68), channel_id=1, source_target_pairs={{0,8},{8,16},{16,24},{24,28},{28,20},{20,12},{12,4},{4,0},{1,9},{9... | collective-permute-start | bytes 393224 | tf_op jit(solution)/shard_map/ppermute | solution.py:263
  79.1 5.0 %collective-permute-start.22 = (f32[128,256]{1,0:T(8,128)S(1)}, f32[128,256]{1,0:T(8,128)S(1)}, u32[]{:S(2)}, u32[]{:S(2)}) collective-permute-start(f32[128,256]{1,0:T(8,128)S(1)} %slice.69), channel_id=1, source_target_pairs={{0,4},{8,0},{16,8},{24,16},{28,24},{20,28},{12,20},{4,12},{1,5},{9... | collective-permute-start | bytes 393224 | tf_op jit(solution)/shard_map/ppermute | solution.py:263

commit v2 on v1

--- a/solution.py
+++ b/solution.py
@@ -28,10 +28,13 @@
 
 
 def mm3(left, right, dims):
-    def one(a, b):
-        return lax.dot_general(a, b, (dims, ((), ())), preferred_element_type=F32)
-
-    return one(left[0], right[0]) + (one(left[0], right[1]) + one(left[1], right[0]))
+    (at_left,), (at_right,) = dims
+    return lax.dot_general(
+        jnp.concatenate([left[0], left[0], left[1]], axis=at_left),
+        jnp.concatenate([right[0], right[1], right[0]], axis=at_right),
+        (dims, ((), ())),
+        preferred_element_type=F32,
+    )
 
 
 def array(shape, dtype=F32):
@@ -154,9 +157,9 @@
                 pltpu.make_async_copy(test_any.at[part], test.at[part], sems.at[1, c]),
             )
         )
-    for a, b in copies:
-        b.start()
-        a.start()
+    for c, (a, b) in enumerate(copies):
+        b.start(priority=int(c > 0))
+        a.start(priority=int(c > 0))
     total = None
     for c, (a, b) in enumerate(copies):
         b.wait()
@@ -176,7 +179,7 @@
 def sketch_parts(snapshot, test_matrix, axis):
     points, depth = snapshot.shape
     width = test_matrix.shape[1]
-    chunks = 8
+    chunks = 2
     half = array((points // 2, width))
     return call(
         functools.partial(sketch_kernel, axis),
@@ -202,6 +205,11 @@
     return lax.axis_index(axis) & 1
 
 
+def join(bit, mine, other):
+    low = bit == 0
+    return jnp.concatenate([jnp.where(low, mine, other), jnp.where(low, other, mine)])
+
+
 def ordered(axis, mine, other):
     low = first_bit(axis) == 0
     return jnp.where(low, mine, other), jnp.where(low, other, mine)
@@ -214,17 +222,25 @@
     scratch[pl.ds(pl.multiple_of((1 - bit) * half, half), half), :] = other_ref[...]
     width = out_ref.shape[1]
     left = scratch[:, pl.ds(pl.multiple_of(bit * width, width), width)]
-    out_ref[:width, :] = mm(left, left, ((0,), (0,)))
     cross = mm(scratch[:, :width], scratch[:, width:], ((0,), (0,)))
-    out_ref[width:, :] = jnp.where(bit == 0, cross[: width // 2], cross[width // 2 :])
+    below = jnp.where(bit == 0, cross[: width // 2], cross[width // 2 :])
+    whole = jnp.concatenate([mm(left, left, ((0,), (0,))), below])
+    share = out_ref.shape[0]
+    out_ref[...] = whole[:share]
+    for n in range(1, whole.shape[0] // share):
+
+        @pl.when((lax.axis_index(axis) >> 1) % (whole.shape[0] // share) == n)
+        def _():
+            out_ref[...] = whole[n * share : (n + 1) * share]
 
 
 def gram_part(mine, other, axis):
     half, width = mine.shape
     block = width // 2
+    shares = 2 if lax.axis_size(axis) % 4 == 0 else 1
     (out,) = call(
         functools.partial(strip_kernel, axis),
-        [array((block + block // 2, block))],
+        [array(((block + block // 2) // shares, block))],
         mine,
         other,
         scratch=[pltpu.VMEM((2 * half, width), F32)],
@@ -343,6 +359,11 @@
 
 
 def body(snapshot, test_matrix):
+    rows, columns = lax.axis_size("rows"), lax.axis_size("cols")
+    whole = snapshot.shape[1] % (128 * rows) == 0 and test_matrix.shape[1] % 256 == 0
+    powers = rows & (rows - 1) == 0 and columns & (columns - 1) == 0
+    if not (whole and powers and rows > 2 and columns > 1):
+        return plain_body(snapshot, test_matrix)
     return steps(snapshot, test_matrix)
 
 
@@ -369,9 +390,12 @@
     while step < ring.length:
         strip = strip + swap(strip, "rows", step)
         step *= 2
+    if columns % 4 == 0:
+        strip = join((lax.axis_index("cols") >> 1) & 1, strip, swap(strip, "cols", 2))
     gram = gram_upper("cols", strip, swap(strip, "cols", 1))
     aheads = [sign * d for d in range(far - 1, 0, -1) for sign in (1, -1)] + [0]
-    parts = products(ring, "cols", aheads, False, stop, srest, top, rest)
+    parts = products(ring, "cols", aheads[:2], False, stop, srest, top, rest)
+    parts += products(ring, "cols", aheads[2:], False, stop, srest, top, rest)
     parts = dict(zip(aheads, parts))
     for d in range(far - 1, 0, -1):
         if d == far - 1:
@@ -412,10 +436,8 @@
 
 
 def solution(mesh):
-    rows = mesh.shape["rows"]
-    ring = rows == 8
     return jax.shard_map(
-        body if ring else plain_body,
+        body,
         mesh=mesh,
         in_specs=(P("rows", "cols"), P("cols", None)),
         out_specs=(P("cols", None), P()),

time: 85.6 us -> 91.9 us (1.074)
  other arithmetic: 1.18 us -> 8.36 us
  starting transfers between devices: 25.4 us -> 23.4 us
  local copies, waits for them, and re-layouts: 0.09 us -> 1.4 us
    ppermute x16, starting transfers between devices: 17.8 us -> 14.4 us  [send(): return lax.ppermute(value, self.axis, pairs)]
    add x3, other arithmetic: 0.09 us -> 2.65 us  [steps(): right = ring.send(parts[d] + right, 1)]
    add x3, other arithmetic: 0.1 us -> 1.74 us  [steps(): left = ring.send(parts[-d] + left, -1)]
    ppermute x16, waiting for transfers between devices: 16.7 us -> 18.4 us  [send(): return lax.ppermute(value, self.axis, pairs)]
    ppermute x7 -> x8, waiting for transfers between devices: 18.1 us -> 16.5 us  [swap(): lax.ppermute(value, axis, [(i, i ^ mask) for i in range(lax.axis_size(axi...]
    add x3, other arithmetic: 0.04 us -> 1.47 us  [steps(): strip = strip + swap(strip, 'rows', step)]
    ppermute x7 -> x8, starting transfers between devices: 7.62 us -> 9.04 us  [swap(): lax.ppermute(value, axis, [(i, i ^ mask) for i in range(lax.axis_size(axi...]
    pallas_call x14 -> x15, Pallas kernels: 22.9 us -> 22.6 us  [call(): pl.pallas_call(kernel, out_shape=outs, in_specs=specs or [VMEM] * len(arg...]
  transfers between devices with their start and end apart: 23 -> 24, of which waited for: 16 -> 17; matrix products, arithmetic and copies ran while one was open for 1% -> 9% of each run, Pallas kernels for 20% -> 19%
where the time goes in v2:
time: 91.9 us; the launch traced here: 91.7 us
  waiting for transfers between devices  34.8 us (38%)
  starting transfers between devices  23.4 us (25%)
  Pallas kernels  22.6 us (25%)
  other arithmetic  8.36 us (9%)
  local copies, waits for them, and re-layouts  1.4 us (2%)
  between operations  1.05 us (1%)
    pallas_call x15, Pallas kernels, call(): pl.pallas_call(kernel, out_shape=outs, in_specs=specs or [VMEM] * len(arg...  22.6 us
    ppermute x16, waiting for transfers between devices, send(): return lax.ppermute(value, self.axis, pairs)  18.4 us
    ppermute x8, waiting for transfers between devices, swap(): lax.ppermute(value, axis, [(i, i ^ mask) for i in range(lax.axis_size(axi...  16.5 us
    ppermute x16, starting transfers between devices, send(): return lax.ppermute(value, self.axis, pairs)  14.4 us
    ppermute x8, starting transfers between devices, swap(): lax.ppermute(value, axis, [(i, i ^ mask) for i in range(lax.axis_size(axi...  9.04 us
    add x3, other arithmetic, steps(): right = ring.send(parts[d] + right, 1)  2.65 us
  transfers between devices with their start and end apart: 24, of which 17 were waited for; matrix products, arithmetic and copies ran while one was open for 9% of the time, Pallas kernels for 19%

profile of v2, /device:TPU:0, one launch (start us, length us, event | category | flops | bytes accessed | tf_op | source)
XLA Modules:
  0.0 91.7 jit_solution(11887106165677063002)
XLA Ops:
  0.6 4.0 %shard_map.41 = (f32[192,256]{1,0:T(8,128)S(1)}, f32[192,256]{1,0:T(8,128)S(1)}, bf16[384,2048]{1,0:T(8,128)(2,1)S(1)}, bf16[384,2048]{1,0:T(8,128)(2,1)S(1)}) custom-call(f32[384,2048]{1,0:T(8,128)} %snap_any.1, f32[2048,256]{1,0:T(8,128)} %test_any.1), custom_call_target="tpu_custom_call" | custom-call | flops 1207959552 | bytes 5242880 | tf_op jit(solution)/shard_map/pallas_call | solution.py:46
  6.3 2.9 %collective-permute-start.1 = (f32[192,256]{1,0:T(8,128)S(1)}, f32[192,256]{1,0:T(8,128)S(1)}, u32[]{:S(2)}, u32[]{:S(2)}) collective-permute-start(f32[192,256]{1,0:T(8,128)S(1)} %add.54), channel_id=1, source_target_pairs={{0,2},{1,3},{2,0},{3,1},{4,6},{5,7},{6,4},{7,5},{8,10},{9,11},{10,... | collective-permute-start | bytes 589832 | tf_op jit(solution)/shard_map/ppermute | solution.py:201
  9.2 5.2 %collective-permute-done.1 = f32[192,256]{1,0:T(8,128)S(1)} collective-permute-done((f32[192,256]{1,0:T(8,128)S(1)}, f32[192,256]{1,0:T(8,128)S(1)}, u32[]{:S(2)}, u32[]{:S(2)}) %collective-permute-start.1) | collective-permute-done | bytes 196640 | tf_op jit(solution)/shard_map/ppermute | solution.py:201
  17.1 1.8 %collective-permute-start.8 = (f32[128,256]{1,0:T(8,128)}, f32[128,256]{1,0:T(8,128)}, u32[]{:S(2)}, u32[]{:S(2)}) collective-permute-start(f32[128,256]{1,0:T(8,128)} %get-tuple-element.31), channel_id=1, source_target_pairs={{0,8},{8,16},{16,24},{24,28},{28,20},{20,12},{12,4},{4,0},{1,9},{9... | collective-permute-start | bytes 393224 | tf_op jit(solution)/shard_map/ppermute | solution.py:279
  19.7 4.2 %collective-permute-done.3 = f32[96,128]{1,0:T(8,128)S(1)} collective-permute-done((f32[96,128]{1,0:T(8,128)S(1)}, f32[96,128]{1,0:T(8,128)S(1)}, u32[]{:S(2)}, u32[]{:S(2)}) %collective-permute-start.3) | collective-permute-done | bytes 49184 | tf_op jit(solution)/shard_map/ppermute | solution.py:201
  26.8 2.6 %collective-permute-done.4 = f32[96,128]{1,0:T(8,128)} collective-permute-done((f32[96,128]{1,0:T(8,128)}, f32[96,128]{1,0:T(8,128)}, u32[]{:S(2)}, u32[]{:S(2)}) %collective-permute-start.4) | collective-permute-done | bytes 49184 | tf_op jit(solution)/shard_map/ppermute | solution.py:201
  30.3 2.3 %collective-permute-start.5 = (f32[96,128]{1,0:T(8,128)S(1)}, f32[96,128]{1,0:T(8,128)S(1)}, u32[]{:S(2)}, u32[]{:S(2)}) collective-permute-start(f32[96,128]{1,0:T(8,128)S(1)} %add.57), channel_id=1, source_target_pairs={{0,16},{4,20},{8,24},{12,28},{16,0},{20,4},{24,8},{28,12},{1,17},{... | collective-permute-start | bytes 147464 | tf_op jit(solution)/shard_map/ppermute | solution.py:201
  32.6 1.6 %pad_add_fusion.1 = f32[256,256]{1,0:T(8,128)} fusion(f32[256,256]{1,0:T(8,128)S(1)} %get-tuple-element.25, f32[128,256]{1,0:T(8,128)} %collective-permute-done.8), kind=kLoop, calls=%fused_computation.6 | loop fusion | flops 65536 | bytes 655360 | tf_op jit(solution)/shard_map/add | solution.py:404
  48.7 3.4 %collective-permute-done.10 = f32[256,256]{1,0:T(8,128)S(1)} collective-permute-done((f32[256,256]{1,0:T(8,128)S(1)}, f32[256,256]{1,0:T(8,128)S(1)}, u32[]{:S(2)}, u32[]{:S(2)}) %collective-permute-start.10) | collective-permute-done | bytes 262176 | tf_op jit(solution)/shard_map/ppermute | solution.py:279
  58.2 1.9 %collective-permute-done.11 = f32[256,256]{1,0:T(8,128)S(1)} collective-permute-done((f32[256,256]{1,0:T(8,128)S(1)}, f32[256,256]{1,0:T(8,128)S(1)}, u32[]{:S(2)}, u32[]{:S(2)}) %collective-permute-start.11) | collective-permute-done | bytes 262176 | tf_op jit(solution)/shard_map/ppermute | solution.py:279
  60.0 1.6 %collective-permute-done.15 = f32[256,256]{1,0:T(8,128)S(1)} collective-permute-done((f32[256,256]{1,0:T(8,128)S(1)}, f32[256,256]{1,0:T(8,128)S(1)}, u32[]{:S(2)}, u32[]{:S(2)}) %collective-permute-start.15) | collective-permute-done | bytes 262176 | tf_op jit(solution)/shard_map/ppermute | solution.py:279
  61.7 1.8 %collective-permute-start.16 = (f32[256,256]{1,0:T(8,128)S(1)}, f32[256,256]{1,0:T(8,128)S(1)}, u32[]{:S(2)}, u32[]{:S(2)}) collective-permute-start(f32[256,256]{1,0:T(8,128)S(1)} %add_add_fusion.refs_8_), channel_id=1, source_target_pairs={{0,8},{8,16},{16,24},{24,28},{28,20},{20,12},{12,4},{4,0},{1,9},{9... | collective-permute-start | bytes 786440 | tf_op jit(solution)/shard_map/ppermute | solution.py:279
  63.8 1.7 %shard_map.46.refs_3_ = f32[32,512]{1,0:T(8,128)S(1)} custom-call(f32[256,256]{1,0:T(8,128)S(1)} %select_maximum_fusion.gram_ref, f32[32,512]{1,0:T(8,128)S(1)} %shard_map.43.refs_0_, f32[32,512]{1,0:T(8,128)S(1)} %shard_map.44.refs_1_, f32[32,512]{1,0:T(8,128)S(1)} %shard_map.45.refs_2_), custom_call_target="tpu_custom_call" | custom-call | flops 25165824 | bytes 458752 | tf_op jit(solution)/shard_map/pallas_call | solution.py:46
  65.5 1.6 %shard_map.47.refs_4_ = f32[32,512]{1,0:T(8,128)S(1)} custom-call(f32[256,256]{1,0:T(8,128)S(1)} %select_maximum_fusion.gram_ref, f32[32,512]{1,0:T(8,128)S(1)} %shard_map.43.refs_0_, f32[32,512]{1,0:T(8,128)S(1)} %shard_map.44.refs_1_, f32[32,512]{1,0:T(8,128)S(1)} %shard_map.45.refs_2_, f32[32,512]{1,0:T(8,128)S(1)} %shard_map.46.refs_3_), custom_call_target="tpu_custom_call" | custom-call | flops 25165824 | bytes 524288 | tf_op jit(solution)/shard_map/pallas_call | solution.py:46
  68.5 1.7 %collective-permute-start.17 = (f32[256,256]{1,0:T(8,128)S(1)}, f32[256,256]{1,0:T(8,128)S(1)}, u32[]{:S(2)}, u32[]{:S(2)}) collective-permute-start(f32[256,256]{1,0:T(8,128)S(1)} %collective-permute-done.16.refs_9_), channel_id=1, source_target_pairs={{0,8},{8,16},{16,24},{24,28},{28,20},{20,12},{12,4},{4,0},{1,9},{9... | collective-permute-start | bytes 786440 | tf_op jit(solution)/shard_map/ppermute | solution.py:279
  70.5 1.8 %shard_map.48.refs_5_ = f32[32,512]{1,0:T(8,128)S(1)} custom-call(f32[256,256]{1,0:T(8,128)S(1)} %select_maximum_fusion.gram_ref, f32[32,512]{1,0:T(8,128)S(1)} %shard_map.43.refs_0_, f32[32,512]{1,0:T(8,128)S(1)} %shard_map.44.refs_1_, f32[32,512]{1,0:T(8,128)S(1)} %shard_map.45.refs_2_, f32[32,512]{1,0:T(8,128)S(1)} %shard_map.46.refs_3_, ...), custom_call_target="tpu_custom_call" | custom-call | flops 25165824 | bytes 589824 | tf_op jit(solution)/shard_map/pallas_call | solution.py:46
  72.3 1.8 %shard_map.49.refs_6_ = f32[32,512]{1,0:T(8,128)S(1)} custom-call(f32[256,256]{1,0:T(8,128)S(1)} %select_maximum_fusion.gram_ref, f32[32,512]{1,0:T(8,128)S(1)} %shard_map.43.refs_0_, f32[32,512]{1,0:T(8,128)S(1)} %shard_map.44.refs_1_, f32[32,512]{1,0:T(8,128)S(1)} %shard_map.45.refs_2_, f32[32,512]{1,0:T(8,128)S(1)} %shard_map.46.refs_3_, ...), custom_call_target="tpu_custom_call" | custom-call | flops 25165824 | bytes 655360 | tf_op jit(solution)/shard_map/pallas_call | solution.py:46
  74.1 1.7 %collective-permute-done.17.refs_11_ = f32[256,256]{1,0:T(8,128)S(1)} collective-permute-done((f32[256,256]{1,0:T(8,128)S(1)}, f32[256,256]{1,0:T(8,128)S(1)}, u32[]{:S(2)}, u32[]{:S(2)}) %collective-permute-start.17) | collective-permute-done | bytes 262176 | tf_op jit(solution)/shard_map/ppermute | solution.py:279
  75.8 1.7 %collective-permute-start.18 = (f32[256,256]{1,0:T(8,128)S(1)}, f32[256,256]{1,0:T(8,128)S(1)}, u32[]{:S(2)}, u32[]{:S(2)}) collective-permute-start(f32[256,256]{1,0:T(8,128)S(1)} %collective-permute-done.17.refs_11_), channel_id=1, source_target_pairs={{0,8},{8,16},{16,24},{24,28},{28,20},{20,12},{12,4},{4,0},{1,9},{9... | collective-permute-start | bytes 786440 | tf_op jit(solution)/shard_map/ppermute | solution.py:279
  77.8 1.9 %shard_map.50.refs_7_ = f32[32,512]{1,0:T(8,128)S(1)} custom-call(f32[256,256]{1,0:T(8,128)S(1)} %select_maximum_fusion.gram_ref, f32[32,512]{1,0:T(8,128)S(1)} %shard_map.43.refs_0_, f32[32,512]{1,0:T(8,128)S(1)} %shard_map.44.refs_1_, f32[32,512]{1,0:T(8,128)S(1)} %shard_map.45.refs_2_, f32[32,512]{1,0:T(8,128)S(1)} %shard_map.46.refs_3_, ...), custom_call_target="tpu_custom_call" | custom-call | flops 25165824 | bytes 720896 | tf_op jit(solution)/shard_map/pallas_call | solution.py:46
  79.7 3.8 %collective-permute-done.18.refs_13_ = f32[256,256]{1,0:T(8,128)S(1)} collective-permute-done((f32[256,256]{1,0:T(8,128)S(1)}, f32[256,256]{1,0:T(8,128)S(1)}, u32[]{:S(2)}, u32[]{:S(2)}) %collective-permute-start.18) | collective-permute-done | bytes 262176 | tf_op jit(solution)/shard_map/ppermute | solution.py:279
  83.6 1.8 %collective-permute-start.19 = (f32[128,256]{1,0:T(8,128)S(1)}, f32[128,256]{1,0:T(8,128)S(1)}, u32[]{:S(2)}, u32[]{:S(2)}) collective-permute-start(f32[128,256]{1,0:T(8,128)S(1)} %slice.68), channel_id=1, source_target_pairs={{0,8},{8,16},{16,24},{24,28},{28,20},{20,12},{12,4},{4,0},{1,9},{9... | collective-permute-start | bytes 393224 | tf_op jit(solution)/shard_map/ppermute | solution.py:279
  86.5 1.8 %shard_map.54.refs_10_ = f32[2048,256]{1,0:T(8,128)} custom-call(f32[32,512]{1,0:T(8,128)S(1)} %shard_map.43.refs_0_, f32[32,512]{1,0:T(8,128)S(1)} %shard_map.44.refs_1_, f32[32,512]{1,0:T(8,128)S(1)} %shard_map.45.refs_2_, f32[32,512]{1,0:T(8,128)S(1)} %shard_map.46.refs_3_, f32[32,512]{1,0:T(8,128)S(1)} %shard_map.47.refs_4_, ...), custom_call_target="tpu_custom_call" | custom-call | flops 704643072 | bytes 2359296 | tf_op jit(solution)/shard_map/pallas_call | solution.py:46
  88.6 1.8 %collective-permute-done.23.refs_9_ = f32[128,256]{1,0:T(8,128)S(1)} collective-permute-done((f32[128,256]{1,0:T(8,128)S(1)}, f32[128,256]{1,0:T(8,128)S(1)}, u32[]{:S(2)}, u32[]{:S(2)}) %collective-permute-start.23) | collective-permute-done | bytes 131104 | tf_op jit(solution)/shard_map/ppermute | solution.py:279
  (80 shorter events, 34.1 us)
Async XLA Ops:
  4.6 1.6 %collective-permute-start = (f32[192,256]{1,0:T(8,128)S(1)}, f32[192,256]{1,0:T(8,128)S(1)}, u32[]{:S(2)}, u32[]{:S(2)}) collective-permute-start(f32[192,256]{1,0:T(8,128)S(1)} %get-tuple-element.17), channel_id=1, source_target_pairs={{0,1},{1,0},{2,3},{3,2},{4,5},{5,4},{6,7},{7,6},{8,9},{9,8},{10,11... | collective-permute-start | bytes 589832 | tf_op jit(solution)/shard_map/ppermute | solution.py:201
  6.3 8.1 %collective-permute-start.1 = (f32[192,256]{1,0:T(8,128)S(1)}, f32[192,256]{1,0:T(8,128)S(1)}, u32[]{:S(2)}, u32[]{:S(2)}) collective-permute-start(f32[192,256]{1,0:T(8,128)S(1)} %add.54), channel_id=1, source_target_pairs={{0,2},{1,3},{2,0},{3,1},{4,6},{5,7},{6,4},{7,5},{8,10},{9,11},{10,... | collective-permute-start | bytes 589832 | tf_op jit(solution)/shard_map/ppermute | solution.py:201
  14.4 1.5 %collective-permute-start.2 = (f32[192,256]{1,0:T(8,128)S(1)}, f32[192,256]{1,0:T(8,128)S(1)}, u32[]{:S(2)}, u32[]{:S(2)}) collective-permute-start(f32[192,256]{1,0:T(8,128)S(1)} %add.55.mine_ref.refs_0_), channel_id=1, source_target_pairs={{0,1},{1,0},{2,3},{3,2},{4,5},{5,4},{6,7},{7,6},{8,9},{9,8},{10,11... | collective-permute-start | bytes 589832 | tf_op jit(solution)/shard_map/ppermute | solution.py:201
  17.1 15.6 %collective-permute-start.8 = (f32[128,256]{1,0:T(8,128)}, f32[128,256]{1,0:T(8,128)}, u32[]{:S(2)}, u32[]{:S(2)}) collective-permute-start(f32[128,256]{1,0:T(8,128)} %get-tuple-element.31), channel_id=1, source_target_pairs={{0,8},{8,16},{16,24},{24,28},{28,20},{20,12},{12,4},{4,0},{1,9},{9... | collective-permute-start | bytes 393224 | tf_op jit(solution)/shard_map/ppermute | solution.py:279
  19.5 4.4 %collective-permute-start.3 = (f32[96,128]{1,0:T(8,128)S(1)}, f32[96,128]{1,0:T(8,128)S(1)}, u32[]{:S(2)}, u32[]{:S(2)}) collective-permute-start(f32[96,128]{1,0:T(8,128)S(1)} %shard_map.42), channel_id=1, source_target_pairs={{0,4},{4,0},{8,12},{12,8},{16,20},{20,16},{24,28},{28,24},{1,5},{5... | collective-permute-start | bytes 147464 | tf_op jit(solution)/shard_map/ppermute | solution.py:201
  24.5 4.9 %collective-permute-start.4 = (f32[96,128]{1,0:T(8,128)}, f32[96,128]{1,0:T(8,128)}, u32[]{:S(2)}, u32[]{:S(2)}) collective-permute-start(f32[96,128]{1,0:T(8,128)} %add.56), channel_id=1, source_target_pairs={{0,8},{4,12},{8,0},{12,4},{16,24},{20,28},{24,16},{28,20},{1,9},{5... | collective-permute-start | bytes 147464 | tf_op jit(solution)/shard_map/ppermute | solution.py:201
  25.8 11.6 %collective-permute-start.12 = (f32[128,256]{1,0:T(8,128)}, f32[128,256]{1,0:T(8,128)S(1)}, u32[]{:S(2)}, u32[]{:S(2)}) collective-permute-start(f32[128,256]{1,0:T(8,128)} %get-tuple-element.30), channel_id=1, source_target_pairs={{0,4},{8,0},{16,8},{24,16},{28,24},{20,28},{12,20},{4,12},{1,5},{9... | collective-permute-start | bytes 393224 | tf_op jit(solution)/shard_map/ppermute | solution.py:279
  30.3 5.5 %collective-permute-start.5 = (f32[96,128]{1,0:T(8,128)S(1)}, f32[96,128]{1,0:T(8,128)S(1)}, u32[]{:S(2)}, u32[]{:S(2)}) collective-permute-start(f32[96,128]{1,0:T(8,128)S(1)} %add.57), channel_id=1, source_target_pairs={{0,16},{4,20},{8,24},{12,28},{16,0},{20,4},{24,8},{28,12},{1,17},{... | collective-permute-start | bytes 147464 | tf_op jit(solution)/shard_map/ppermute | solution.py:201
  34.3 8.1 %collective-permute-start.9 = (f32[256,256]{1,0:T(8,128)}, f32[256,256]{1,0:T(8,128)}, u32[]{:S(2)}, u32[]{:S(2)}) collective-permute-start(f32[256,256]{1,0:T(8,128)} %pad_add_fusion.1), channel_id=1, source_target_pairs={{0,8},{8,16},{16,24},{24,28},{28,20},{20,12},{12,4},{4,0},{1,9},{9... | collective-permute-start | bytes 786440 | tf_op jit(solution)/shard_map/ppermute | solution.py:279
  35.8 4.2 %collective-permute-start.6 = (f32[96,128]{1,0:T(8,128)S(1)}, f32[96,128]{1,0:T(8,128)S(1)}, u32[]{:S(2)}, u32[]{:S(2)}) collective-permute-start(f32[96,128]{1,0:T(8,128)S(1)} %add.58), channel_id=1, source_target_pairs={{0,2},{1,3},{2,0},{3,1},{4,6},{5,7},{6,4},{7,5},{8,10},{9,11},{10,... | collective-permute-start | bytes 147464 | tf_op jit(solution)/shard_map/ppermute | solution.py:201
  38.2 6.7 %collective-permute-start.13 = (f32[256,256]{1,0:T(8,128)}, f32[256,256]{1,0:T(8,128)}, u32[]{:S(2)}, u32[]{:S(2)}) collective-permute-start(f32[256,256]{1,0:T(8,128)} %pad_add_fusion), channel_id=1, source_target_pairs={{0,4},{8,0},{16,8},{24,16},{28,24},{20,28},{12,20},{4,12},{1,5},{9... | collective-permute-start | bytes 786440 | tf_op jit(solution)/shard_map/ppermute | solution.py:279
  41.3 5.3 %collective-permute-start.7 = (f32[192,128]{1,0:T(8,128)}, f32[192,128]{1,0:T(8,128)}, u32[]{:S(2)}, u32[]{:S(2)}) collective-permute-start(f32[192,128]{1,0:T(8,128)} %pad_maximum_fusion), channel_id=1, source_target_pairs={{0,1},{1,0},{2,3},{3,2},{4,5},{5,4},{6,7},{7,6},{8,9},{9,8},{10,11... | collective-permute-start | bytes 294920 | tf_op jit(solution)/shard_map/ppermute | solution.py:201
  43.4 8.7 %collective-permute-start.10 = (f32[256,256]{1,0:T(8,128)S(1)}, f32[256,256]{1,0:T(8,128)S(1)}, u32[]{:S(2)}, u32[]{:S(2)}) collective-permute-start(f32[256,256]{1,0:T(8,128)S(1)} %add.60), channel_id=1, source_target_pairs={{0,8},{8,16},{16,24},{24,28},{28,20},{20,12},{12,4},{4,0},{1,9},{9... | collective-permute-start | bytes 786440 | tf_op jit(solution)/shard_map/ppermute | solution.py:279
  45.8 8.2 %collective-permute-start.14 = (f32[256,256]{1,0:T(8,128)S(1)}, f32[256,256]{1,0:T(8,128)S(1)}, u32[]{:S(2)}, u32[]{:S(2)}) collective-permute-start(f32[256,256]{1,0:T(8,128)S(1)} %add.63), channel_id=1, source_target_pairs={{0,4},{8,0},{16,8},{24,16},{28,24},{20,28},{12,20},{4,12},{1,5},{9... | collective-permute-start | bytes 786440 | tf_op jit(solution)/shard_map/ppermute | solution.py:279
  52.2 7.9 %collective-permute-start.11 = (f32[256,256]{1,0:T(8,128)S(1)}, f32[256,256]{1,0:T(8,128)S(1)}, u32[]{:S(2)}, u32[]{:S(2)}) collective-permute-start(f32[256,256]{1,0:T(8,128)S(1)} %add.61), channel_id=1, source_target_pairs={{0,8},{8,16},{16,24},{24,28},{28,20},{20,12},{12,4},{4,0},{1,9},{9... | collective-permute-start | bytes 786440 | tf_op jit(solution)/shard_map/ppermute | solution.py:279
  54.1 7.6 %collective-permute-start.15 = (f32[256,256]{1,0:T(8,128)S(1)}, f32[256,256]{1,0:T(8,128)S(1)}, u32[]{:S(2)}, u32[]{:S(2)}) collective-permute-start(f32[256,256]{1,0:T(8,128)S(1)} %add.64), channel_id=1, source_target_pairs={{0,4},{8,0},{16,8},{24,16},{28,24},{20,28},{12,20},{4,12},{1,5},{9... | collective-permute-start | bytes 786440 | tf_op jit(solution)/shard_map/ppermute | solution.py:279
  61.7 6.7 %collective-permute-start.16 = (f32[256,256]{1,0:T(8,128)S(1)}, f32[256,256]{1,0:T(8,128)S(1)}, u32[]{:S(2)}, u32[]{:S(2)}) collective-permute-start(f32[256,256]{1,0:T(8,128)S(1)} %add_add_fusion.refs_8_), channel_id=1, source_target_pairs={{0,8},{8,16},{16,24},{24,28},{28,20},{20,12},{12,4},{4,0},{1,9},{9... | collective-permute-start | bytes 786440 | tf_op jit(solution)/shard_map/ppermute | solution.py:279
  63.5 6.7 %collective-permute-start.20 = (f32[256,256]{1,0:T(8,128)S(1)}, f32[256,256]{1,0:T(8,128)S(1)}, u32[]{:S(2)}, u32[]{:S(2)}) collective-permute-start(f32[256,256]{1,0:T(8,128)S(1)} %add_add_fusion.refs_8_), channel_id=1, source_target_pairs={{0,4},{8,0},{16,8},{24,16},{28,24},{20,28},{12,20},{4,12},{1,5},{9... | collective-permute-start | bytes 786440 | tf_op jit(solution)/shard_map/ppermute | solution.py:279
  68.5 7.3 %collective-permute-start.17 = (f32[256,256]{1,0:T(8,128)S(1)}, f32[256,256]{1,0:T(8,128)S(1)}, u32[]{:S(2)}, u32[]{:S(2)}) collective-permute-start(f32[256,256]{1,0:T(8,128)S(1)} %collective-permute-done.16.refs_9_), channel_id=1, source_target_pairs={{0,8},{8,16},{16,24},{24,28},{28,20},{20,12},{12,4},{4,0},{1,9},{9... | collective-permute-start | bytes 786440 | tf_op jit(solution)/shard_map/ppermute | solution.py:279
  70.2 7.3 %collective-permute-start.21 = (f32[256,256]{1,0:T(8,128)S(1)}, f32[256,256]{1,0:T(8,128)S(1)}, u32[]{:S(2)}, u32[]{:S(2)}) collective-permute-start(f32[256,256]{1,0:T(8,128)S(1)} %collective-permute-done.20.refs_10_), channel_id=1, source_target_pairs={{0,4},{8,0},{16,8},{24,16},{28,24},{20,28},{12,20},{4,12},{1,5},{9... | collective-permute-start | bytes 786440 | tf_op jit(solution)/shard_map/ppermute | solution.py:279
  75.8 7.8 %collective-permute-start.18 = (f32[256,256]{1,0:T(8,128)S(1)}, f32[256,256]{1,0:T(8,128)S(1)}, u32[]{:S(2)}, u32[]{:S(2)}) collective-permute-start(f32[256,256]{1,0:T(8,128)S(1)} %collective-permute-done.17.refs_11_), channel_id=1, source_target_pairs={{0,8},{8,16},{16,24},{24,28},{28,20},{20,12},{12,4},{4,0},{1,9},{9... | collective-permute-start | bytes 786440 | tf_op jit(solution)/shard_map/ppermute | solution.py:279
  77.5 7.8 %collective-permute-start.22 = (f32[256,256]{1,0:T(8,128)S(1)}, f32[256,256]{1,0:T(8,128)S(1)}, u32[]{:S(2)}, u32[]{:S(2)}) collective-permute-start(f32[256,256]{1,0:T(8,128)S(1)} %collective-permute-done.21.refs_12_), channel_id=1, source_target_pairs={{0,4},{8,0},{16,8},{24,16},{28,24},{20,28},{12,20},{4,12},{1,5},{9... | collective-permute-start | bytes 786440 | tf_op jit(solution)/shard_map/ppermute | solution.py:279
  83.6 5.0 %collective-permute-start.19 = (f32[128,256]{1,0:T(8,128)S(1)}, f32[128,256]{1,0:T(8,128)S(1)}, u32[]{:S(2)}, u32[]{:S(2)}) collective-permute-start(f32[128,256]{1,0:T(8,128)S(1)} %slice.68), channel_id=1, source_target_pairs={{0,8},{8,16},{16,24},{24,28},{28,20},{20,12},{12,4},{4,0},{1,9},{9... | collective-permute-start | bytes 393224 | tf_op jit(solution)/shard_map/ppermute | solution.py:279
  85.4 5.0 %collective-permute-start.23 = (f32[128,256]{1,0:T(8,128)S(1)}, f32[128,256]{1,0:T(8,128)S(1)}, u32[]{:S(2)}, u32[]{:S(2)}) collective-permute-start(f32[128,256]{1,0:T(8,128)S(1)} %slice.69), channel_id=1, source_target_pairs={{0,4},{8,0},{16,8},{24,16},{28,24},{20,28},{12,20},{4,12},{1,5},{9... | collective-permute-start | bytes 393224 | tf_op jit(solution)/shard_map/ppermute | solution.py:279
  (4 other events, 12.4 us)

commit v3 on v2

--- a/solution.py
+++ b/solution.py
@@ -371,11 +371,16 @@
     mine, other, top, rest = sketch_parts(snapshot, test_matrix, "cols")
     columns = lax.axis_size("cols")
     mine = mine + swap(other, "cols", 1)
+    mid = mine.shape[0] // 2
     mask = 2
     while mask < columns:
-        mine = mine + swap(mine, "cols", mask)
+        pieces = [swap(mine[:mid], "cols", mask), swap(mine[mid:], "cols", mask)]
+        pieces = [mine[:mid] + pieces[0], mine[mid:] + pieces[1]]
         mask *= 2
-    other = swap(mine, "cols", 1)
+        if mask < columns:
+            mine = jnp.concatenate(pieces)
+    others = [swap(piece, "cols", 1) for piece in pieces]
+    mine, other = jnp.concatenate(pieces), jnp.concatenate(others)
 
     ring = Ring("rows")
     far = ring.length // 2

time: 91.9 us -> 92 us (level)
    ppermute x8 -> x10, waiting for transfers between devices: 16.5 us -> 16.8 us  [swap(): lax.ppermute(value, axis, [(i, i ^ mask) for i in range(lax.axis_size(axi...]
    ppermute x8 -> x10, starting transfers between devices: 9.04 us -> 9.1 us  [swap(): lax.ppermute(value, axis, [(i, i ^ mask) for i in range(lax.axis_size(axi...]
  transfers between devices with their start and end apart: 24 -> 26, of which waited for: 17 -> 19; matrix products, arithmetic and copies ran while one was open for 9% -> 9% of each run, Pallas kernels for 19% -> 19%
where the time goes in v3:
time: 92 us; the launch traced here: 91.7 us
  waiting for transfers between devices  35 us (38%)
  starting transfers between devices  23.3 us (25%)
  Pallas kernels  22.6 us (25%)
  other arithmetic  8.35 us (9%)
  local copies, waits for them, and re-layouts  1.43 us (2%)
  between operations  1.06 us (1%)
    pallas_call x15, Pallas kernels, call(): pl.pallas_call(kernel, out_shape=outs, in_specs=specs or [VMEM] * len(arg...  22.6 us
    ppermute x16, waiting for transfers between devices, send(): return lax.ppermute(value, self.axis, pairs)  18.2 us
    ppermute x10, waiting for transfers between devices, swap(): lax.ppermute(value, axis, [(i, i ^ mask) for i in range(lax.axis_size(axi...  16.8 us
    ppermute x16, starting transfers between devices, send(): return lax.ppermute(value, self.axis, pairs)  14.2 us
    ppermute x10, starting transfers between devices, swap(): lax.ppermute(value, axis, [(i, i ^ mask) for i in range(lax.axis_size(axi...  9.1 us
    add x3, other arithmetic, steps(): right = ring.send(parts[d] + right, 1)  2.65 us
  transfers between devices with their start and end apart: 26, of which 19 were waited for; matrix products, arithmetic and copies ran while one was open for 9% of the time, Pallas kernels for 19%

profile of v3, /device:TPU:0, one launch (start us, length us, event | category | flops | bytes accessed | tf_op | source)
XLA Modules:
  0.0 91.7 jit_solution(9038238806628846224)
XLA Ops:
  0.6 4.0 %shard_map.41 = (f32[192,256]{1,0:T(8,128)S(1)}, f32[192,256]{1,0:T(8,128)S(1)}, bf16[384,2048]{1,0:T(8,128)(2,1)S(1)}, bf16[384,2048]{1,0:T(8,128)(2,1)S(1)}) custom-call(f32[384,2048]{1,0:T(8,128)} %snap_any.1, f32[2048,256]{1,0:T(8,128)} %test_any.1), custom_call_target="tpu_custom_call" | custom-call | flops 1207959552 | bytes 5242880 | tf_op jit(solution)/shard_map/pallas_call | solution.py:46
  6.3 2.9 %collective-permute-start.1 = (f32[96,256]{1,0:T(8,128)S(1)}, f32[96,256]{1,0:T(8,128)S(1)}, u32[]{:S(2)}, u32[]{:S(2)}) collective-permute-start(f32[96,256]{1,0:T(8,128)S(1)} %get-tuple-element.36), channel_id=1, source_target_pairs={{0,2},{1,3},{2,0},{3,1},{4,6},{5,7},{6,4},{7,5},{8,10},{9,11},{10,... | collective-permute-start | bytes 294920 | tf_op jit(solution)/shard_map/ppermute | solution.py:201
  9.3 3.6 %collective-permute-done.1 = f32[96,256]{1,0:T(8,128)S(1)} collective-permute-done((f32[96,256]{1,0:T(8,128)S(1)}, f32[96,256]{1,0:T(8,128)S(1)}, u32[]{:S(2)}, u32[]{:S(2)}) %collective-permute-start.1) | collective-permute-done | bytes 98336 | tf_op jit(solution)/shard_map/ppermute | solution.py:201
  17.1 1.8 %collective-permute-start.10 = (f32[128,256]{1,0:T(8,128)}, f32[128,256]{1,0:T(8,128)}, u32[]{:S(2)}, u32[]{:S(2)}) collective-permute-start(f32[128,256]{1,0:T(8,128)} %get-tuple-element.31), channel_id=1, source_target_pairs={{0,8},{8,16},{16,24},{24,28},{28,20},{20,12},{12,4},{4,0},{1,9},{9... | collective-permute-start | bytes 393224 | tf_op jit(solution)/shard_map/ppermute | solution.py:279
  19.8 4.4 %collective-permute-done.5 = f32[96,128]{1,0:T(8,128)S(1)} collective-permute-done((f32[96,128]{1,0:T(8,128)S(1)}, f32[96,128]{1,0:T(8,128)S(1)}, u32[]{:S(2)}, u32[]{:S(2)}) %collective-permute-start.5) | collective-permute-done | bytes 49184 | tf_op jit(solution)/shard_map/ppermute | solution.py:201
  26.9 2.9 %collective-permute-done.6 = f32[96,128]{1,0:T(8,128)} collective-permute-done((f32[96,128]{1,0:T(8,128)}, f32[96,128]{1,0:T(8,128)}, u32[]{:S(2)}, u32[]{:S(2)}) %collective-permute-start.6) | collective-permute-done | bytes 49184 | tf_op jit(solution)/shard_map/ppermute | solution.py:201
  30.6 2.1 %collective-permute-start.7 = (f32[96,128]{1,0:T(8,128)S(1)}, f32[96,128]{1,0:T(8,128)S(1)}, u32[]{:S(2)}, u32[]{:S(2)}) collective-permute-start(f32[96,128]{1,0:T(8,128)S(1)} %add.61), channel_id=1, source_target_pairs={{0,16},{4,20},{8,24},{12,28},{16,0},{20,4},{24,8},{28,12},{1,17},{... | collective-permute-start | bytes 147464 | tf_op jit(solution)/shard_map/ppermute | solution.py:201
  32.7 1.6 %pad_add_fusion.1 = f32[256,256]{1,0:T(8,128)} fusion(f32[256,256]{1,0:T(8,128)S(1)} %get-tuple-element.25, f32[128,256]{1,0:T(8,128)} %collective-permute-done.10), kind=kLoop, calls=%fused_computation.6 | loop fusion | flops 65536 | bytes 655360 | tf_op jit(solution)/shard_map/add | solution.py:409
  38.6 1.6 %collective-permute-done.8 = f32[96,128]{1,0:T(8,128)S(1)} collective-permute-done((f32[96,128]{1,0:T(8,128)S(1)}, f32[96,128]{1,0:T(8,128)S(1)}, u32[]{:S(2)}, u32[]{:S(2)}) %collective-permute-start.8) | collective-permute-done | bytes 49184 | tf_op jit(solution)/shard_map/ppermute | solution.py:201
  49.0 3.4 %collective-permute-done.12 = f32[256,256]{1,0:T(8,128)S(1)} collective-permute-done((f32[256,256]{1,0:T(8,128)S(1)}, f32[256,256]{1,0:T(8,128)S(1)}, u32[]{:S(2)}, u32[]{:S(2)}) %collective-permute-start.12) | collective-permute-done | bytes 262176 | tf_op jit(solution)/shard_map/ppermute | solution.py:279
  58.4 1.9 %collective-permute-done.13 = f32[256,256]{1,0:T(8,128)S(1)} collective-permute-done((f32[256,256]{1,0:T(8,128)S(1)}, f32[256,256]{1,0:T(8,128)S(1)}, u32[]{:S(2)}, u32[]{:S(2)}) %collective-permute-start.13) | collective-permute-done | bytes 262176 | tf_op jit(solution)/shard_map/ppermute | solution.py:279
  61.8 1.8 %collective-permute-start.18 = (f32[256,256]{1,0:T(8,128)S(1)}, f32[256,256]{1,0:T(8,128)S(1)}, u32[]{:S(2)}, u32[]{:S(2)}) collective-permute-start(f32[256,256]{1,0:T(8,128)S(1)} %add_add_fusion.refs_8_), channel_id=1, source_target_pairs={{0,8},{8,16},{16,24},{24,28},{28,20},{20,12},{12,4},{4,0},{1,9},{9... | collective-permute-start | bytes 786440 | tf_op jit(solution)/shard_map/ppermute | solution.py:279
  63.8 1.7 %shard_map.46.refs_3_ = f32[32,512]{1,0:T(8,128)S(1)} custom-call(f32[256,256]{1,0:T(8,128)S(1)} %select_maximum_fusion.gram_ref, f32[32,512]{1,0:T(8,128)S(1)} %shard_map.43.refs_0_, f32[32,512]{1,0:T(8,128)S(1)} %shard_map.44.refs_1_, f32[32,512]{1,0:T(8,128)S(1)} %shard_map.45.refs_2_), custom_call_target="tpu_custom_call" | custom-call | flops 25165824 | bytes 458752 | tf_op jit(solution)/shard_map/pallas_call | solution.py:46
  65.5 1.6 %shard_map.47.refs_4_ = f32[32,512]{1,0:T(8,128)S(1)} custom-call(f32[256,256]{1,0:T(8,128)S(1)} %select_maximum_fusion.gram_ref, f32[32,512]{1,0:T(8,128)S(1)} %shard_map.43.refs_0_, f32[32,512]{1,0:T(8,128)S(1)} %shard_map.44.refs_1_, f32[32,512]{1,0:T(8,128)S(1)} %shard_map.45.refs_2_, f32[32,512]{1,0:T(8,128)S(1)} %shard_map.46.refs_3_), custom_call_target="tpu_custom_call" | custom-call | flops 25165824 | bytes 524288 | tf_op jit(solution)/shard_map/pallas_call | solution.py:46
  68.5 1.7 %collective-permute-start.19 = (f32[256,256]{1,0:T(8,128)S(1)}, f32[256,256]{1,0:T(8,128)S(1)}, u32[]{:S(2)}, u32[]{:S(2)}) collective-permute-start(f32[256,256]{1,0:T(8,128)S(1)} %collective-permute-done.18.refs_9_), channel_id=1, source_target_pairs={{0,8},{8,16},{16,24},{24,28},{28,20},{20,12},{12,4},{4,0},{1,9},{9... | collective-permute-start | bytes 786440 | tf_op jit(solution)/shard_map/ppermute | solution.py:279
  70.6 1.8 %shard_map.48.refs_5_ = f32[32,512]{1,0:T(8,128)S(1)} custom-call(f32[256,256]{1,0:T(8,128)S(1)} %select_maximum_fusion.gram_ref, f32[32,512]{1,0:T(8,128)S(1)} %shard_map.43.refs_0_, f32[32,512]{1,0:T(8,128)S(1)} %shard_map.44.refs_1_, f32[32,512]{1,0:T(8,128)S(1)} %shard_map.45.refs_2_, f32[32,512]{1,0:T(8,128)S(1)} %shard_map.46.refs_3_, ...), custom_call_target="tpu_custom_call" | custom-call | flops 25165824 | bytes 589824 | tf_op jit(solution)/shard_map/pallas_call | solution.py:46
  72.3 1.8 %shard_map.49.refs_6_ = f32[32,512]{1,0:T(8,128)S(1)} custom-call(f32[256,256]{1,0:T(8,128)S(1)} %select_maximum_fusion.gram_ref, f32[32,512]{1,0:T(8,128)S(1)} %shard_map.43.refs_0_, f32[32,512]{1,0:T(8,128)S(1)} %shard_map.44.refs_1_, f32[32,512]{1,0:T(8,128)S(1)} %shard_map.45.refs_2_, f32[32,512]{1,0:T(8,128)S(1)} %shard_map.46.refs_3_, ...), custom_call_target="tpu_custom_call" | custom-call | flops 25165824 | bytes 655360 | tf_op jit(solution)/shard_map/pallas_call | solution.py:46
  74.2 1.7 %collective-permute-done.19.refs_11_ = f32[256,256]{1,0:T(8,128)S(1)} collective-permute-done((f32[256,256]{1,0:T(8,128)S(1)}, f32[256,256]{1,0:T(8,128)S(1)}, u32[]{:S(2)}, u32[]{:S(2)}) %collective-permute-start.19) | collective-permute-done | bytes 262176 | tf_op jit(solution)/shard_map/ppermute | solution.py:279
  75.8 1.7 %collective-permute-start.20 = (f32[256,256]{1,0:T(8,128)S(1)}, f32[256,256]{1,0:T(8,128)S(1)}, u32[]{:S(2)}, u32[]{:S(2)}) collective-permute-start(f32[256,256]{1,0:T(8,128)S(1)} %collective-permute-done.19.refs_11_), channel_id=1, source_target_pairs={{0,8},{8,16},{16,24},{24,28},{28,20},{20,12},{12,4},{4,0},{1,9},{9... | collective-permute-start | bytes 786440 | tf_op jit(solution)/shard_map/ppermute | solution.py:279
  77.8 1.9 %shard_map.50.refs_7_ = f32[32,512]{1,0:T(8,128)S(1)} custom-call(f32[256,256]{1,0:T(8,128)S(1)} %select_maximum_fusion.gram_ref, f32[32,512]{1,0:T(8,128)S(1)} %shard_map.43.refs_0_, f32[32,512]{1,0:T(8,128)S(1)} %shard_map.44.refs_1_, f32[32,512]{1,0:T(8,128)S(1)} %shard_map.45.refs_2_, f32[32,512]{1,0:T(8,128)S(1)} %shard_map.46.refs_3_, ...), custom_call_target="tpu_custom_call" | custom-call | flops 25165824 | bytes 720896 | tf_op jit(solution)/shard_map/pallas_call | solution.py:46
  79.7 3.8 %collective-permute-done.20.refs_13_ = f32[256,256]{1,0:T(8,128)S(1)} collective-permute-done((f32[256,256]{1,0:T(8,128)S(1)}, f32[256,256]{1,0:T(8,128)S(1)}, u32[]{:S(2)}, u32[]{:S(2)}) %collective-permute-start.20) | collective-permute-done | bytes 262176 | tf_op jit(solution)/shard_map/ppermute | solution.py:279
  83.6 1.8 %collective-permute-start.21 = (f32[128,256]{1,0:T(8,128)S(1)}, f32[128,256]{1,0:T(8,128)S(1)}, u32[]{:S(2)}, u32[]{:S(2)}) collective-permute-start(f32[128,256]{1,0:T(8,128)S(1)} %slice.80), channel_id=1, source_target_pairs={{0,8},{8,16},{16,24},{24,28},{28,20},{20,12},{12,4},{4,0},{1,9},{9... | collective-permute-start | bytes 393224 | tf_op jit(solution)/shard_map/ppermute | solution.py:279
  86.6 1.8 %shard_map.54.refs_10_ = f32[2048,256]{1,0:T(8,128)} custom-call(f32[32,512]{1,0:T(8,128)S(1)} %shard_map.43.refs_0_, f32[32,512]{1,0:T(8,128)S(1)} %shard_map.44.refs_1_, f32[32,512]{1,0:T(8,128)S(1)} %shard_map.45.refs_2_, f32[32,512]{1,0:T(8,128)S(1)} %shard_map.46.refs_3_, f32[32,512]{1,0:T(8,128)S(1)} %shard_map.47.refs_4_, ...), custom_call_target="tpu_custom_call" | custom-call | flops 704643072 | bytes 2359296 | tf_op jit(solution)/shard_map/pallas_call | solution.py:46
  88.6 1.8 %collective-permute-done.25.refs_9_ = f32[128,256]{1,0:T(8,128)S(1)} collective-permute-done((f32[128,256]{1,0:T(8,128)S(1)}, f32[128,256]{1,0:T(8,128)S(1)}, u32[]{:S(2)}, u32[]{:S(2)}) %collective-permute-start.25) | collective-permute-done | bytes 131104 | tf_op jit(solution)/shard_map/ppermute | solution.py:279
  (88 shorter events, 35.5 us)
Async XLA Ops:
  4.6 1.6 %collective-permute-start = (f32[192,256]{1,0:T(8,128)S(1)}, f32[192,256]{1,0:T(8,128)S(1)}, u32[]{:S(2)}, u32[]{:S(2)}) collective-permute-start(f32[192,256]{1,0:T(8,128)S(1)} %get-tuple-element.17), channel_id=1, source_target_pairs={{0,1},{1,0},{2,3},{3,2},{4,5},{5,4},{6,7},{7,6},{8,9},{9,8},{10,11... | collective-permute-start | bytes 589832 | tf_op jit(solution)/shard_map/ppermute | solution.py:201
  6.3 6.6 %collective-permute-start.1 = (f32[96,256]{1,0:T(8,128)S(1)}, f32[96,256]{1,0:T(8,128)S(1)}, u32[]{:S(2)}, u32[]{:S(2)}) collective-permute-start(f32[96,256]{1,0:T(8,128)S(1)} %get-tuple-element.36), channel_id=1, source_target_pairs={{0,2},{1,3},{2,0},{3,1},{4,6},{5,7},{6,4},{7,5},{8,10},{9,11},{10,... | collective-permute-start | bytes 294920 | tf_op jit(solution)/shard_map/ppermute | solution.py:201
  9.2 5.2 %collective-permute-start.2 = (f32[96,256]{1,0:T(8,128)S(1)}, f32[96,256]{1,0:T(8,128)S(1)}, u32[]{:S(2)}, u32[]{:S(2)}) collective-permute-start(f32[96,256]{1,0:T(8,128)S(1)} %get-tuple-element.37), channel_id=1, source_target_pairs={{0,2},{1,3},{2,0},{3,1},{4,6},{5,7},{6,4},{7,5},{8,10},{9,11},{10,... | collective-permute-start | bytes 294920 | tf_op jit(solution)/shard_map/ppermute | solution.py:201
  17.1 15.5 %collective-permute-start.10 = (f32[128,256]{1,0:T(8,128)}, f32[128,256]{1,0:T(8,128)}, u32[]{:S(2)}, u32[]{:S(2)}) collective-permute-start(f32[128,256]{1,0:T(8,128)} %get-tuple-element.31), channel_id=1, source_target_pairs={{0,8},{8,16},{16,24},{24,28},{28,20},{20,12},{12,4},{4,0},{1,9},{9... | collective-permute-start | bytes 393224 | tf_op jit(solution)/shard_map/ppermute | solution.py:279
  19.5 4.6 %collective-permute-start.5 = (f32[96,128]{1,0:T(8,128)S(1)}, f32[96,128]{1,0:T(8,128)S(1)}, u32[]{:S(2)}, u32[]{:S(2)}) collective-permute-start(f32[96,128]{1,0:T(8,128)S(1)} %shard_map.42), channel_id=1, source_target_pairs={{0,4},{4,0},{8,12},{12,8},{16,20},{20,16},{24,28},{28,24},{1,5},{5... | collective-permute-start | bytes 147464 | tf_op jit(solution)/shard_map/ppermute | solution.py:201
  24.8 4.9 %collective-permute-start.6 = (f32[96,128]{1,0:T(8,128)}, f32[96,128]{1,0:T(8,128)}, u32[]{:S(2)}, u32[]{:S(2)}) collective-permute-start(f32[96,128]{1,0:T(8,128)} %add.60), channel_id=1, source_target_pairs={{0,8},{4,12},{8,0},{12,4},{16,24},{20,28},{24,16},{28,20},{1,9},{5... | collective-permute-start | bytes 147464 | tf_op jit(solution)/shard_map/ppermute | solution.py:201
  25.9 11.8 %collective-permute-start.14 = (f32[128,256]{1,0:T(8,128)}, f32[128,256]{1,0:T(8,128)S(1)}, u32[]{:S(2)}, u32[]{:S(2)}) collective-permute-start(f32[128,256]{1,0:T(8,128)} %get-tuple-element.30), channel_id=1, source_target_pairs={{0,4},{8,0},{16,8},{24,16},{28,24},{20,28},{12,20},{4,12},{1,5},{9... | collective-permute-start | bytes 393224 | tf_op jit(solution)/shard_map/ppermute | solution.py:279
  30.6 5.5 %collective-permute-start.7 = (f32[96,128]{1,0:T(8,128)S(1)}, f32[96,128]{1,0:T(8,128)S(1)}, u32[]{:S(2)}, u32[]{:S(2)}) collective-permute-start(f32[96,128]{1,0:T(8,128)S(1)} %add.61), channel_id=1, source_target_pairs={{0,16},{4,20},{8,24},{12,28},{16,0},{20,4},{24,8},{28,12},{1,17},{... | collective-permute-start | bytes 147464 | tf_op jit(solution)/shard_map/ppermute | solution.py:201
  34.3 8.3 %collective-permute-start.11 = (f32[256,256]{1,0:T(8,128)}, f32[256,256]{1,0:T(8,128)}, u32[]{:S(2)}, u32[]{:S(2)}) collective-permute-start(f32[256,256]{1,0:T(8,128)} %pad_add_fusion.1), channel_id=1, source_target_pairs={{0,8},{8,16},{16,24},{24,28},{28,20},{20,12},{12,4},{4,0},{1,9},{9... | collective-permute-start | bytes 786440 | tf_op jit(solution)/shard_map/ppermute | solution.py:279
  36.1 4.2 %collective-permute-start.8 = (f32[96,128]{1,0:T(8,128)S(1)}, f32[96,128]{1,0:T(8,128)S(1)}, u32[]{:S(2)}, u32[]{:S(2)}) collective-permute-start(f32[96,128]{1,0:T(8,128)S(1)} %add.62), channel_id=1, source_target_pairs={{0,2},{1,3},{2,0},{3,1},{4,6},{5,7},{6,4},{7,5},{8,10},{9,11},{10,... | collective-permute-start | bytes 147464 | tf_op jit(solution)/shard_map/ppermute | solution.py:201
  38.4 6.7 %collective-permute-start.15 = (f32[256,256]{1,0:T(8,128)}, f32[256,256]{1,0:T(8,128)}, u32[]{:S(2)}, u32[]{:S(2)}) collective-permute-start(f32[256,256]{1,0:T(8,128)} %pad_add_fusion), channel_id=1, source_target_pairs={{0,4},{8,0},{16,8},{24,16},{28,24},{20,28},{12,20},{4,12},{1,5},{9... | collective-permute-start | bytes 786440 | tf_op jit(solution)/shard_map/ppermute | solution.py:279
  41.5 5.3 %collective-permute-start.9 = (f32[192,128]{1,0:T(8,128)}, f32[192,128]{1,0:T(8,128)}, u32[]{:S(2)}, u32[]{:S(2)}) collective-permute-start(f32[192,128]{1,0:T(8,128)} %pad_maximum_fusion.1), channel_id=1, source_target_pairs={{0,1},{1,0},{2,3},{3,2},{4,5},{5,4},{6,7},{7,6},{8,9},{9,8},{10,11... | collective-permute-start | bytes 294920 | tf_op jit(solution)/shard_map/ppermute | solution.py:201
  43.6 8.8 %collective-permute-start.12 = (f32[256,256]{1,0:T(8,128)S(1)}, f32[256,256]{1,0:T(8,128)S(1)}, u32[]{:S(2)}, u32[]{:S(2)}) collective-permute-start(f32[256,256]{1,0:T(8,128)S(1)} %add.64), channel_id=1, source_target_pairs={{0,8},{8,16},{16,24},{24,28},{28,20},{20,12},{12,4},{4,0},{1,9},{9... | collective-permute-start | bytes 786440 | tf_op jit(solution)/shard_map/ppermute | solution.py:279
  46.0 8.0 %collective-permute-start.16 = (f32[256,256]{1,0:T(8,128)S(1)}, f32[256,256]{1,0:T(8,128)S(1)}, u32[]{:S(2)}, u32[]{:S(2)}) collective-permute-start(f32[256,256]{1,0:T(8,128)S(1)} %add.67), channel_id=1, source_target_pairs={{0,4},{8,0},{16,8},{24,16},{28,24},{20,28},{12,20},{4,12},{1,5},{9... | collective-permute-start | bytes 786440 | tf_op jit(solution)/shard_map/ppermute | solution.py:279
  52.4 7.9 %collective-permute-start.13 = (f32[256,256]{1,0:T(8,128)S(1)}, f32[256,256]{1,0:T(8,128)S(1)}, u32[]{:S(2)}, u32[]{:S(2)}) collective-permute-start(f32[256,256]{1,0:T(8,128)S(1)} %add.65), channel_id=1, source_target_pairs={{0,8},{8,16},{16,24},{24,28},{28,20},{20,12},{12,4},{4,0},{1,9},{9... | collective-permute-start | bytes 786440 | tf_op jit(solution)/shard_map/ppermute | solution.py:279
  54.1 7.6 %collective-permute-start.17 = (f32[256,256]{1,0:T(8,128)S(1)}, f32[256,256]{1,0:T(8,128)S(1)}, u32[]{:S(2)}, u32[]{:S(2)}) collective-permute-start(f32[256,256]{1,0:T(8,128)S(1)} %add.68), channel_id=1, source_target_pairs={{0,4},{8,0},{16,8},{24,16},{28,24},{20,28},{12,20},{4,12},{1,5},{9... | collective-permute-start | bytes 786440 | tf_op jit(solution)/shard_map/ppermute | solution.py:279
  61.8 6.8 %collective-permute-start.18 = (f32[256,256]{1,0:T(8,128)S(1)}, f32[256,256]{1,0:T(8,128)S(1)}, u32[]{:S(2)}, u32[]{:S(2)}) collective-permute-start(f32[256,256]{1,0:T(8,128)S(1)} %add_add_fusion.refs_8_), channel_id=1, source_target_pairs={{0,8},{8,16},{16,24},{24,28},{28,20},{20,12},{12,4},{4,0},{1,9},{9... | collective-permute-start | bytes 786440 | tf_op jit(solution)/shard_map/ppermute | solution.py:279
  63.6 6.7 %collective-permute-start.22 = (f32[256,256]{1,0:T(8,128)S(1)}, f32[256,256]{1,0:T(8,128)S(1)}, u32[]{:S(2)}, u32[]{:S(2)}) collective-permute-start(f32[256,256]{1,0:T(8,128)S(1)} %add_add_fusion.refs_8_), channel_id=1, source_target_pairs={{0,4},{8,0},{16,8},{24,16},{28,24},{20,28},{12,20},{4,12},{1,5},{9... | collective-permute-start | bytes 786440 | tf_op jit(solution)/shard_map/ppermute | solution.py:279
  68.5 7.3 %collective-permute-start.19 = (f32[256,256]{1,0:T(8,128)S(1)}, f32[256,256]{1,0:T(8,128)S(1)}, u32[]{:S(2)}, u32[]{:S(2)}) collective-permute-start(f32[256,256]{1,0:T(8,128)S(1)} %collective-permute-done.18.refs_9_), channel_id=1, source_target_pairs={{0,8},{8,16},{16,24},{24,28},{28,20},{20,12},{12,4},{4,0},{1,9},{9... | collective-permute-start | bytes 786440 | tf_op jit(solution)/shard_map/ppermute | solution.py:279
  70.3 7.3 %collective-permute-start.23 = (f32[256,256]{1,0:T(8,128)S(1)}, f32[256,256]{1,0:T(8,128)S(1)}, u32[]{:S(2)}, u32[]{:S(2)}) collective-permute-start(f32[256,256]{1,0:T(8,128)S(1)} %collective-permute-done.22.refs_10_), channel_id=1, source_target_pairs={{0,4},{8,0},{16,8},{24,16},{28,24},{20,28},{12,20},{4,12},{1,5},{9... | collective-permute-start | bytes 786440 | tf_op jit(solution)/shard_map/ppermute | solution.py:279
  75.8 7.8 %collective-permute-start.20 = (f32[256,256]{1,0:T(8,128)S(1)}, f32[256,256]{1,0:T(8,128)S(1)}, u32[]{:S(2)}, u32[]{:S(2)}) collective-permute-start(f32[256,256]{1,0:T(8,128)S(1)} %collective-permute-done.19.refs_11_), channel_id=1, source_target_pairs={{0,8},{8,16},{16,24},{24,28},{28,20},{20,12},{12,4},{4,0},{1,9},{9... | collective-permute-start | bytes 786440 | tf_op jit(solution)/shard_map/ppermute | solution.py:279
  77.6 7.8 %collective-permute-start.24 = (f32[256,256]{1,0:T(8,128)S(1)}, f32[256,256]{1,0:T(8,128)S(1)}, u32[]{:S(2)}, u32[]{:S(2)}) collective-permute-start(f32[256,256]{1,0:T(8,128)S(1)} %collective-permute-done.23.refs_12_), channel_id=1, source_target_pairs={{0,4},{8,0},{16,8},{24,16},{28,24},{20,28},{12,20},{4,12},{1,5},{9... | collective-permute-start | bytes 786440 | tf_op jit(solution)/shard_map/ppermute | solution.py:279
  83.6 5.0 %collective-permute-start.21 = (f32[128,256]{1,0:T(8,128)S(1)}, f32[128,256]{1,0:T(8,128)S(1)}, u32[]{:S(2)}, u32[]{:S(2)}) collective-permute-start(f32[128,256]{1,0:T(8,128)S(1)} %slice.80), channel_id=1, source_target_pairs={{0,8},{8,16},{16,24},{24,28},{28,20},{20,12},{12,4},{4,0},{1,9},{9... | collective-permute-start | bytes 393224 | tf_op jit(solution)/shard_map/ppermute | solution.py:279
  85.4 5.0 %collective-permute-start.25 = (f32[128,256]{1,0:T(8,128)S(1)}, f32[128,256]{1,0:T(8,128)S(1)}, u32[]{:S(2)}, u32[]{:S(2)}) collective-permute-start(f32[128,256]{1,0:T(8,128)S(1)} %slice.81), channel_id=1, source_target_pairs={{0,4},{8,0},{16,8},{24,16},{28,24},{20,28},{12,20},{4,12},{1,5},{9... | collective-permute-start | bytes 393224 | tf_op jit(solution)/shard_map/ppermute | solution.py:279
  (6 other events, 15.2 us)

commit v4 on v3

--- a/solution.py
+++ b/solution.py
@@ -14,6 +14,7 @@
 F32, BF16 = jnp.float32, jnp.bfloat16
 MIB = 1 << 20
 PANEL = 32
+FIRST = 4
 
 
 def mm(left, right, dims, precision=high):
@@ -146,11 +147,11 @@
 
 def sketch_kernel(axis, snap_any, test_any, mine_ref, other_ref, top_ref, rest_ref, snap, test, sems):
     depth = snap.shape[1]
-    chunks = sems.shape[1]
-    size = depth // chunks
+    first = depth * FIRST // 16
+    parts = ((0, first), (first, depth - first))
     copies = []
-    for c in range(chunks):
-        part = pl.ds(c * size, size)
+    for c, (start, size) in enumerate(parts):
+        part = pl.ds(start, size)
         copies.append(
             (
                 pltpu.make_async_copy(snap_any.at[:, part], snap.at[:, part], sems.at[0, c]),
@@ -164,7 +165,7 @@
     for c, (a, b) in enumerate(copies):
         b.wait()
         a.wait()
-        part = slice(c * size, (c + 1) * size)
+        part = slice(parts[c][0], sum(parts[c]))
         left = split(snap[:, part])
         top_ref[:, part], rest_ref[:, part] = left
         term = mm3(left, split(test[part, :]), ((1,), (0,)))

time: 92 us -> 92 us (level)
  no operation moved by 1% of the time
where the time goes in v4:
time: 92 us; the launch traced here: 91.7 us
  waiting for transfers between devices  35 us (38%)
  starting transfers between devices  23.3 us (25%)
  Pallas kernels  22.6 us (25%)
  other arithmetic  8.35 us (9%)
  local copies, waits for them, and re-layouts  1.43 us (2%)
  between operations  1.06 us (1%)
    pallas_call x15, Pallas kernels, call(): pl.pallas_call(kernel, out_shape=outs, in_specs=specs or [VMEM] * len(arg...  22.6 us
    ppermute x16, waiting for transfers between devices, send(): return lax.ppermute(value, self.axis, pairs)  18.2 us
    ppermute x10, waiting for transfers between devices, swap(): lax.ppermute(value, axis, [(i, i ^ mask) for i in range(lax.axis_size(axi...  16.8 us
    ppermute x16, starting transfers between devices, send(): return lax.ppermute(value, self.axis, pairs)  14.2 us
    ppermute x10, starting transfers between devices, swap(): lax.ppermute(value, axis, [(i, i ^ mask) for i in range(lax.axis_size(axi...  9.11 us
    add x3, other arithmetic, steps(): right = ring.send(parts[d] + right, 1)  2.65 us
  transfers between devices with their start and end apart: 26, of which 19 were waited for; matrix products, arithmetic and copies ran while one was open for 9% of the time, Pallas kernels for 19%

profile of v4, /device:TPU:0, one launch (start us, length us, event | category | flops | bytes accessed | tf_op | source)
XLA Modules:
  0.0 91.7 jit_solution(15011578568936468066)
XLA Ops:
  0.6 4.0 %shard_map.41 = (f32[192,256]{1,0:T(8,128)S(1)}, f32[192,256]{1,0:T(8,128)S(1)}, bf16[384,2048]{1,0:T(8,128)(2,1)S(1)}, bf16[384,2048]{1,0:T(8,128)(2,1)S(1)}) custom-call(f32[384,2048]{1,0:T(8,128)} %snap_any.1, f32[2048,256]{1,0:T(8,128)} %test_any.1), custom_call_target="tpu_custom_call" | custom-call | flops 1207959552 | bytes 5242880 | tf_op jit(solution)/shard_map/pallas_call | solution.py:47
  6.3 2.9 %collective-permute-start.1 = (f32[96,256]{1,0:T(8,128)S(1)}, f32[96,256]{1,0:T(8,128)S(1)}, u32[]{:S(2)}, u32[]{:S(2)}) collective-permute-start(f32[96,256]{1,0:T(8,128)S(1)} %get-tuple-element.36), channel_id=1, source_target_pairs={{0,2},{1,3},{2,0},{3,1},{4,6},{5,7},{6,4},{7,5},{8,10},{9,11},{10,... | collective-permute-start | bytes 294920 | tf_op jit(solution)/shard_map/ppermute | solution.py:202
  9.3 3.6 %collective-permute-done.1 = f32[96,256]{1,0:T(8,128)S(1)} collective-permute-done((f32[96,256]{1,0:T(8,128)S(1)}, f32[96,256]{1,0:T(8,128)S(1)}, u32[]{:S(2)}, u32[]{:S(2)}) %collective-permute-start.1) | collective-permute-done | bytes 98336 | tf_op jit(solution)/shard_map/ppermute | solution.py:202
  17.1 1.8 %collective-permute-start.10 = (f32[128,256]{1,0:T(8,128)}, f32[128,256]{1,0:T(8,128)}, u32[]{:S(2)}, u32[]{:S(2)}) collective-permute-start(f32[128,256]{1,0:T(8,128)} %get-tuple-element.31), channel_id=1, source_target_pairs={{0,8},{8,16},{16,24},{24,28},{28,20},{20,12},{12,4},{4,0},{1,9},{9... | collective-permute-start | bytes 393224 | tf_op jit(solution)/shard_map/ppermute | solution.py:280
  19.8 4.4 %collective-permute-done.5 = f32[96,128]{1,0:T(8,128)S(1)} collective-permute-done((f32[96,128]{1,0:T(8,128)S(1)}, f32[96,128]{1,0:T(8,128)S(1)}, u32[]{:S(2)}, u32[]{:S(2)}) %collective-permute-start.5) | collective-permute-done | bytes 49184 | tf_op jit(solution)/shard_map/ppermute | solution.py:202
  26.9 2.9 %collective-permute-done.6 = f32[96,128]{1,0:T(8,128)} collective-permute-done((f32[96,128]{1,0:T(8,128)}, f32[96,128]{1,0:T(8,128)}, u32[]{:S(2)}, u32[]{:S(2)}) %collective-permute-start.6) | collective-permute-done | bytes 49184 | tf_op jit(solution)/shard_map/ppermute | solution.py:202
  30.5 2.1 %collective-permute-start.7 = (f32[96,128]{1,0:T(8,128)S(1)}, f32[96,128]{1,0:T(8,128)S(1)}, u32[]{:S(2)}, u32[]{:S(2)}) collective-permute-start(f32[96,128]{1,0:T(8,128)S(1)} %add.61), channel_id=1, source_target_pairs={{0,16},{4,20},{8,24},{12,28},{16,0},{20,4},{24,8},{28,12},{1,17},{... | collective-permute-start | bytes 147464 | tf_op jit(solution)/shard_map/ppermute | solution.py:202
  32.6 1.6 %pad_add_fusion.1 = f32[256,256]{1,0:T(8,128)} fusion(f32[256,256]{1,0:T(8,128)S(1)} %get-tuple-element.25, f32[128,256]{1,0:T(8,128)} %collective-permute-done.10), kind=kLoop, calls=%fused_computation.6 | loop fusion | flops 65536 | bytes 655360 | tf_op jit(solution)/shard_map/add | solution.py:410
  38.6 1.6 %collective-permute-done.8 = f32[96,128]{1,0:T(8,128)S(1)} collective-permute-done((f32[96,128]{1,0:T(8,128)S(1)}, f32[96,128]{1,0:T(8,128)S(1)}, u32[]{:S(2)}, u32[]{:S(2)}) %collective-permute-start.8) | collective-permute-done | bytes 49184 | tf_op jit(solution)/shard_map/ppermute | solution.py:202
  48.9 3.4 %collective-permute-done.12 = f32[256,256]{1,0:T(8,128)S(1)} collective-permute-done((f32[256,256]{1,0:T(8,128)S(1)}, f32[256,256]{1,0:T(8,128)S(1)}, u32[]{:S(2)}, u32[]{:S(2)}) %collective-permute-start.12) | collective-permute-done | bytes 262176 | tf_op jit(solution)/shard_map/ppermute | solution.py:280
  58.4 1.9 %collective-permute-done.13 = f32[256,256]{1,0:T(8,128)S(1)} collective-permute-done((f32[256,256]{1,0:T(8,128)S(1)}, f32[256,256]{1,0:T(8,128)S(1)}, u32[]{:S(2)}, u32[]{:S(2)}) %collective-permute-start.13) | collective-permute-done | bytes 262176 | tf_op jit(solution)/shard_map/ppermute | solution.py:280
  61.8 1.8 %collective-permute-start.18 = (f32[256,256]{1,0:T(8,128)S(1)}, f32[256,256]{1,0:T(8,128)S(1)}, u32[]{:S(2)}, u32[]{:S(2)}) collective-permute-start(f32[256,256]{1,0:T(8,128)S(1)} %add_add_fusion.refs_8_), channel_id=1, source_target_pairs={{0,8},{8,16},{16,24},{24,28},{28,20},{20,12},{12,4},{4,0},{1,9},{9... | collective-permute-start | bytes 786440 | tf_op jit(solution)/shard_map/ppermute | solution.py:280
  63.8 1.7 %shard_map.46.refs_3_ = f32[32,512]{1,0:T(8,128)S(1)} custom-call(f32[256,256]{1,0:T(8,128)S(1)} %select_maximum_fusion.gram_ref, f32[32,512]{1,0:T(8,128)S(1)} %shard_map.43.refs_0_, f32[32,512]{1,0:T(8,128)S(1)} %shard_map.44.refs_1_, f32[32,512]{1,0:T(8,128)S(1)} %shard_map.45.refs_2_), custom_call_target="tpu_custom_call" | custom-call | flops 25165824 | bytes 458752 | tf_op jit(solution)/shard_map/pallas_call | solution.py:47
  65.5 1.6 %shard_map.47.refs_4_ = f32[32,512]{1,0:T(8,128)S(1)} custom-call(f32[256,256]{1,0:T(8,128)S(1)} %select_maximum_fusion.gram_ref, f32[32,512]{1,0:T(8,128)S(1)} %shard_map.43.refs_0_, f32[32,512]{1,0:T(8,128)S(1)} %shard_map.44.refs_1_, f32[32,512]{1,0:T(8,128)S(1)} %shard_map.45.refs_2_, f32[32,512]{1,0:T(8,128)S(1)} %shard_map.46.refs_3_), custom_call_target="tpu_custom_call" | custom-call | flops 25165824 | bytes 524288 | tf_op jit(solution)/shard_map/pallas_call | solution.py:47
  68.5 1.7 %collective-permute-start.19 = (f32[256,256]{1,0:T(8,128)S(1)}, f32[256,256]{1,0:T(8,128)S(1)}, u32[]{:S(2)}, u32[]{:S(2)}) collective-permute-start(f32[256,256]{1,0:T(8,128)S(1)} %collective-permute-done.18.refs_9_), channel_id=1, source_target_pairs={{0,8},{8,16},{16,24},{24,28},{28,20},{20,12},{12,4},{4,0},{1,9},{9... | collective-permute-start | bytes 786440 | tf_op jit(solution)/shard_map/ppermute | solution.py:280
  70.5 1.8 %shard_map.48.refs_5_ = f32[32,512]{1,0:T(8,128)S(1)} custom-call(f32[256,256]{1,0:T(8,128)S(1)} %select_maximum_fusion.gram_ref, f32[32,512]{1,0:T(8,128)S(1)} %shard_map.43.refs_0_, f32[32,512]{1,0:T(8,128)S(1)} %shard_map.44.refs_1_, f32[32,512]{1,0:T(8,128)S(1)} %shard_map.45.refs_2_, f32[32,512]{1,0:T(8,128)S(1)} %shard_map.46.refs_3_, ...), custom_call_target="tpu_custom_call" | custom-call | flops 25165824 | bytes 589824 | tf_op jit(solution)/shard_map/pallas_call | solution.py:47
  72.3 1.8 %shard_map.49.refs_6_ = f32[32,512]{1,0:T(8,128)S(1)} custom-call(f32[256,256]{1,0:T(8,128)S(1)} %select_maximum_fusion.gram_ref, f32[32,512]{1,0:T(8,128)S(1)} %shard_map.43.refs_0_, f32[32,512]{1,0:T(8,128)S(1)} %shard_map.44.refs_1_, f32[32,512]{1,0:T(8,128)S(1)} %shard_map.45.refs_2_, f32[32,512]{1,0:T(8,128)S(1)} %shard_map.46.refs_3_, ...), custom_call_target="tpu_custom_call" | custom-call | flops 25165824 | bytes 655360 | tf_op jit(solution)/shard_map/pallas_call | solution.py:47
  74.1 1.7 %collective-permute-done.19.refs_11_ = f32[256,256]{1,0:T(8,128)S(1)} collective-permute-done((f32[256,256]{1,0:T(8,128)S(1)}, f32[256,256]{1,0:T(8,128)S(1)}, u32[]{:S(2)}, u32[]{:S(2)}) %collective-permute-start.19) | collective-permute-done | bytes 262176 | tf_op jit(solution)/shard_map/ppermute | solution.py:280
  75.8 1.7 %collective-permute-start.20 = (f32[256,256]{1,0:T(8,128)S(1)}, f32[256,256]{1,0:T(8,128)S(1)}, u32[]{:S(2)}, u32[]{:S(2)}) collective-permute-start(f32[256,256]{1,0:T(8,128)S(1)} %collective-permute-done.19.refs_11_), channel_id=1, source_target_pairs={{0,8},{8,16},{16,24},{24,28},{28,20},{20,12},{12,4},{4,0},{1,9},{9... | collective-permute-start | bytes 786440 | tf_op jit(solution)/shard_map/ppermute | solution.py:280
  77.8 1.9 %shard_map.50.refs_7_ = f32[32,512]{1,0:T(8,128)S(1)} custom-call(f32[256,256]{1,0:T(8,128)S(1)} %select_maximum_fusion.gram_ref, f32[32,512]{1,0:T(8,128)S(1)} %shard_map.43.refs_0_, f32[32,512]{1,0:T(8,128)S(1)} %shard_map.44.refs_1_, f32[32,512]{1,0:T(8,128)S(1)} %shard_map.45.refs_2_, f32[32,512]{1,0:T(8,128)S(1)} %shard_map.46.refs_3_, ...), custom_call_target="tpu_custom_call" | custom-call | flops 25165824 | bytes 720896 | tf_op jit(solution)/shard_map/pallas_call | solution.py:47
  79.7 3.8 %collective-permute-done.20.refs_13_ = f32[256,256]{1,0:T(8,128)S(1)} collective-permute-done((f32[256,256]{1,0:T(8,128)S(1)}, f32[256,256]{1,0:T(8,128)S(1)}, u32[]{:S(2)}, u32[]{:S(2)}) %collective-permute-start.20) | collective-permute-done | bytes 262176 | tf_op jit(solution)/shard_map/ppermute | solution.py:280
  83.6 1.8 %collective-permute-start.21 = (f32[128,256]{1,0:T(8,128)S(1)}, f32[128,256]{1,0:T(8,128)S(1)}, u32[]{:S(2)}, u32[]{:S(2)}) collective-permute-start(f32[128,256]{1,0:T(8,128)S(1)} %slice.80), channel_id=1, source_target_pairs={{0,8},{8,16},{16,24},{24,28},{28,20},{20,12},{12,4},{4,0},{1,9},{9... | collective-permute-start | bytes 393224 | tf_op jit(solution)/shard_map/ppermute | solution.py:280
  86.5 1.8 %shard_map.54.refs_10_ = f32[2048,256]{1,0:T(8,128)} custom-call(f32[32,512]{1,0:T(8,128)S(1)} %shard_map.43.refs_0_, f32[32,512]{1,0:T(8,128)S(1)} %shard_map.44.refs_1_, f32[32,512]{1,0:T(8,128)S(1)} %shard_map.45.refs_2_, f32[32,512]{1,0:T(8,128)S(1)} %shard_map.46.refs_3_, f32[32,512]{1,0:T(8,128)S(1)} %shard_map.47.refs_4_, ...), custom_call_target="tpu_custom_call" | custom-call | flops 704643072 | bytes 2359296 | tf_op jit(solution)/shard_map/pallas_call | solution.py:47
  88.6 1.8 %collective-permute-done.25.refs_9_ = f32[128,256]{1,0:T(8,128)S(1)} collective-permute-done((f32[128,256]{1,0:T(8,128)S(1)}, f32[128,256]{1,0:T(8,128)S(1)}, u32[]{:S(2)}, u32[]{:S(2)}) %collective-permute-start.25) | collective-permute-done | bytes 131104 | tf_op jit(solution)/shard_map/ppermute | solution.py:280
  (88 shorter events, 35.5 us)
Async XLA Ops:
  4.6 1.6 %collective-permute-start = (f32[192,256]{1,0:T(8,128)S(1)}, f32[192,256]{1,0:T(8,128)S(1)}, u32[]{:S(2)}, u32[]{:S(2)}) collective-permute-start(f32[192,256]{1,0:T(8,128)S(1)} %get-tuple-element.17), channel_id=1, source_target_pairs={{0,1},{1,0},{2,3},{3,2},{4,5},{5,4},{6,7},{7,6},{8,9},{9,8},{10,11... | collective-permute-start | bytes 589832 | tf_op jit(solution)/shard_map/ppermute | solution.py:202
  6.3 6.6 %collective-permute-start.1 = (f32[96,256]{1,0:T(8,128)S(1)}, f32[96,256]{1,0:T(8,128)S(1)}, u32[]{:S(2)}, u32[]{:S(2)}) collective-permute-start(f32[96,256]{1,0:T(8,128)S(1)} %get-tuple-element.36), channel_id=1, source_target_pairs={{0,2},{1,3},{2,0},{3,1},{4,6},{5,7},{6,4},{7,5},{8,10},{9,11},{10,... | collective-permute-start | bytes 294920 | tf_op jit(solution)/shard_map/ppermute | solution.py:202
  9.2 5.2 %collective-permute-start.2 = (f32[96,256]{1,0:T(8,128)S(1)}, f32[96,256]{1,0:T(8,128)S(1)}, u32[]{:S(2)}, u32[]{:S(2)}) collective-permute-start(f32[96,256]{1,0:T(8,128)S(1)} %get-tuple-element.37), channel_id=1, source_target_pairs={{0,2},{1,3},{2,0},{3,1},{4,6},{5,7},{6,4},{7,5},{8,10},{9,11},{10,... | collective-permute-start | bytes 294920 | tf_op jit(solution)/shard_map/ppermute | solution.py:202
  17.1 15.5 %collective-permute-start.10 = (f32[128,256]{1,0:T(8,128)}, f32[128,256]{1,0:T(8,128)}, u32[]{:S(2)}, u32[]{:S(2)}) collective-permute-start(f32[128,256]{1,0:T(8,128)} %get-tuple-element.31), channel_id=1, source_target_pairs={{0,8},{8,16},{16,24},{24,28},{28,20},{20,12},{12,4},{4,0},{1,9},{9... | collective-permute-start | bytes 393224 | tf_op jit(solution)/shard_map/ppermute | solution.py:280
  19.5 4.7 %collective-permute-start.5 = (f32[96,128]{1,0:T(8,128)S(1)}, f32[96,128]{1,0:T(8,128)S(1)}, u32[]{:S(2)}, u32[]{:S(2)}) collective-permute-start(f32[96,128]{1,0:T(8,128)S(1)} %shard_map.42), channel_id=1, source_target_pairs={{0,4},{4,0},{8,12},{12,8},{16,20},{20,16},{24,28},{28,24},{1,5},{5... | collective-permute-start | bytes 147464 | tf_op jit(solution)/shard_map/ppermute | solution.py:202
  24.8 4.9 %collective-permute-start.6 = (f32[96,128]{1,0:T(8,128)}, f32[96,128]{1,0:T(8,128)}, u32[]{:S(2)}, u32[]{:S(2)}) collective-permute-start(f32[96,128]{1,0:T(8,128)} %add.60), channel_id=1, source_target_pairs={{0,8},{4,12},{8,0},{12,4},{16,24},{20,28},{24,16},{28,20},{1,9},{5... | collective-permute-start | bytes 147464 | tf_op jit(solution)/shard_map/ppermute | solution.py:202
  25.9 11.8 %collective-permute-start.14 = (f32[128,256]{1,0:T(8,128)}, f32[128,256]{1,0:T(8,128)S(1)}, u32[]{:S(2)}, u32[]{:S(2)}) collective-permute-start(f32[128,256]{1,0:T(8,128)} %get-tuple-element.30), channel_id=1, source_target_pairs={{0,4},{8,0},{16,8},{24,16},{28,24},{20,28},{12,20},{4,12},{1,5},{9... | collective-permute-start | bytes 393224 | tf_op jit(solution)/shard_map/ppermute | solution.py:280
  30.5 5.5 %collective-permute-start.7 = (f32[96,128]{1,0:T(8,128)S(1)}, f32[96,128]{1,0:T(8,128)S(1)}, u32[]{:S(2)}, u32[]{:S(2)}) collective-permute-start(f32[96,128]{1,0:T(8,128)S(1)} %add.61), channel_id=1, source_target_pairs={{0,16},{4,20},{8,24},{12,28},{16,0},{20,4},{24,8},{28,12},{1,17},{... | collective-permute-start | bytes 147464 | tf_op jit(solution)/shard_map/ppermute | solution.py:202
  34.3 8.3 %collective-permute-start.11 = (f32[256,256]{1,0:T(8,128)}, f32[256,256]{1,0:T(8,128)}, u32[]{:S(2)}, u32[]{:S(2)}) collective-permute-start(f32[256,256]{1,0:T(8,128)} %pad_add_fusion.1), channel_id=1, source_target_pairs={{0,8},{8,16},{16,24},{24,28},{28,20},{20,12},{12,4},{4,0},{1,9},{9... | collective-permute-start | bytes 786440 | tf_op jit(solution)/shard_map/ppermute | solution.py:280
  36.1 4.2 %collective-permute-start.8 = (f32[96,128]{1,0:T(8,128)S(1)}, f32[96,128]{1,0:T(8,128)S(1)}, u32[]{:S(2)}, u32[]{:S(2)}) collective-permute-start(f32[96,128]{1,0:T(8,128)S(1)} %add.62), channel_id=1, source_target_pairs={{0,2},{1,3},{2,0},{3,1},{4,6},{5,7},{6,4},{7,5},{8,10},{9,11},{10,... | collective-permute-start | bytes 147464 | tf_op jit(solution)/shard_map/ppermute | solution.py:202
  38.4 6.7 %collective-permute-start.15 = (f32[256,256]{1,0:T(8,128)}, f32[256,256]{1,0:T(8,128)}, u32[]{:S(2)}, u32[]{:S(2)}) collective-permute-start(f32[256,256]{1,0:T(8,128)} %pad_add_fusion), channel_id=1, source_target_pairs={{0,4},{8,0},{16,8},{24,16},{28,24},{20,28},{12,20},{4,12},{1,5},{9... | collective-permute-start | bytes 786440 | tf_op jit(solution)/shard_map/ppermute | solution.py:280
  41.5 5.2 %collective-permute-start.9 = (f32[192,128]{1,0:T(8,128)}, f32[192,128]{1,0:T(8,128)}, u32[]{:S(2)}, u32[]{:S(2)}) collective-permute-start(f32[192,128]{1,0:T(8,128)} %pad_maximum_fusion.1), channel_id=1, source_target_pairs={{0,1},{1,0},{2,3},{3,2},{4,5},{5,4},{6,7},{7,6},{8,9},{9,8},{10,11... | collective-permute-start | bytes 294920 | tf_op jit(solution)/shard_map/ppermute | solution.py:202
  43.6 8.8 %collective-permute-start.12 = (f32[256,256]{1,0:T(8,128)S(1)}, f32[256,256]{1,0:T(8,128)S(1)}, u32[]{:S(2)}, u32[]{:S(2)}) collective-permute-start(f32[256,256]{1,0:T(8,128)S(1)} %add.64), channel_id=1, source_target_pairs={{0,8},{8,16},{16,24},{24,28},{28,20},{20,12},{12,4},{4,0},{1,9},{9... | collective-permute-start | bytes 786440 | tf_op jit(solution)/shard_map/ppermute | solution.py:280
  46.0 8.0 %collective-permute-start.16 = (f32[256,256]{1,0:T(8,128)S(1)}, f32[256,256]{1,0:T(8,128)S(1)}, u32[]{:S(2)}, u32[]{:S(2)}) collective-permute-start(f32[256,256]{1,0:T(8,128)S(1)} %add.67), channel_id=1, source_target_pairs={{0,4},{8,0},{16,8},{24,16},{28,24},{20,28},{12,20},{4,12},{1,5},{9... | collective-permute-start | bytes 786440 | tf_op jit(solution)/shard_map/ppermute | solution.py:280
  52.4 7.9 %collective-permute-start.13 = (f32[256,256]{1,0:T(8,128)S(1)}, f32[256,256]{1,0:T(8,128)S(1)}, u32[]{:S(2)}, u32[]{:S(2)}) collective-permute-start(f32[256,256]{1,0:T(8,128)S(1)} %add.65), channel_id=1, source_target_pairs={{0,8},{8,16},{16,24},{24,28},{28,20},{20,12},{12,4},{4,0},{1,9},{9... | collective-permute-start | bytes 786440 | tf_op jit(solution)/shard_map/ppermute | solution.py:280
  54.1 7.6 %collective-permute-start.17 = (f32[256,256]{1,0:T(8,128)S(1)}, f32[256,256]{1,0:T(8,128)S(1)}, u32[]{:S(2)}, u32[]{:S(2)}) collective-permute-start(f32[256,256]{1,0:T(8,128)S(1)} %add.68), channel_id=1, source_target_pairs={{0,4},{8,0},{16,8},{24,16},{28,24},{20,28},{12,20},{4,12},{1,5},{9... | collective-permute-start | bytes 786440 | tf_op jit(solution)/shard_map/ppermute | solution.py:280
  61.8 6.8 %collective-permute-start.18 = (f32[256,256]{1,0:T(8,128)S(1)}, f32[256,256]{1,0:T(8,128)S(1)}, u32[]{:S(2)}, u32[]{:S(2)}) collective-permute-start(f32[256,256]{1,0:T(8,128)S(1)} %add_add_fusion.refs_8_), channel_id=1, source_target_pairs={{0,8},{8,16},{16,24},{24,28},{28,20},{20,12},{12,4},{4,0},{1,9},{9... | collective-permute-start | bytes 786440 | tf_op jit(solution)/shard_map/ppermute | solution.py:280
  63.5 6.7 %collective-permute-start.22 = (f32[256,256]{1,0:T(8,128)S(1)}, f32[256,256]{1,0:T(8,128)S(1)}, u32[]{:S(2)}, u32[]{:S(2)}) collective-permute-start(f32[256,256]{1,0:T(8,128)S(1)} %add_add_fusion.refs_8_), channel_id=1, source_target_pairs={{0,4},{8,0},{16,8},{24,16},{28,24},{20,28},{12,20},{4,12},{1,5},{9... | collective-permute-start | bytes 786440 | tf_op jit(solution)/shard_map/ppermute | solution.py:280
  68.5 7.3 %collective-permute-start.19 = (f32[256,256]{1,0:T(8,128)S(1)}, f32[256,256]{1,0:T(8,128)S(1)}, u32[]{:S(2)}, u32[]{:S(2)}) collective-permute-start(f32[256,256]{1,0:T(8,128)S(1)} %collective-permute-done.18.refs_9_), channel_id=1, source_target_pairs={{0,8},{8,16},{16,24},{24,28},{28,20},{20,12},{12,4},{4,0},{1,9},{9... | collective-permute-start | bytes 786440 | tf_op jit(solution)/shard_map/ppermute | solution.py:280
  70.3 7.3 %collective-permute-start.23 = (f32[256,256]{1,0:T(8,128)S(1)}, f32[256,256]{1,0:T(8,128)S(1)}, u32[]{:S(2)}, u32[]{:S(2)}) collective-permute-start(f32[256,256]{1,0:T(8,128)S(1)} %collective-permute-done.22.refs_10_), channel_id=1, source_target_pairs={{0,4},{8,0},{16,8},{24,16},{28,24},{20,28},{12,20},{4,12},{1,5},{9... | collective-permute-start | bytes 786440 | tf_op jit(solution)/shard_map/ppermute | solution.py:280
  75.8 7.8 %collective-permute-start.20 = (f32[256,256]{1,0:T(8,128)S(1)}, f32[256,256]{1,0:T(8,128)S(1)}, u32[]{:S(2)}, u32[]{:S(2)}) collective-permute-start(f32[256,256]{1,0:T(8,128)S(1)} %collective-permute-done.19.refs_11_), channel_id=1, source_target_pairs={{0,8},{8,16},{16,24},{24,28},{28,20},{20,12},{12,4},{4,0},{1,9},{9... | collective-permute-start | bytes 786440 | tf_op jit(solution)/shard_map/ppermute | solution.py:280
  77.5 7.8 %collective-permute-start.24 = (f32[256,256]{1,0:T(8,128)S(1)}, f32[256,256]{1,0:T(8,128)S(1)}, u32[]{:S(2)}, u32[]{:S(2)}) collective-permute-start(f32[256,256]{1,0:T(8,128)S(1)} %collective-permute-done.23.refs_12_), channel_id=1, source_target_pairs={{0,4},{8,0},{16,8},{24,16},{28,24},{20,28},{12,20},{4,12},{1,5},{9... | collective-permute-start | bytes 786440 | tf_op jit(solution)/shard_map/ppermute | solution.py:280
  83.6 5.0 %collective-permute-start.21 = (f32[128,256]{1,0:T(8,128)S(1)}, f32[128,256]{1,0:T(8,128)S(1)}, u32[]{:S(2)}, u32[]{:S(2)}) collective-permute-start(f32[128,256]{1,0:T(8,128)S(1)} %slice.80), channel_id=1, source_target_pairs={{0,8},{8,16},{16,24},{24,28},{28,20},{20,12},{12,4},{4,0},{1,9},{9... | collective-permute-start | bytes 393224 | tf_op jit(solution)/shard_map/ppermute | solution.py:280
  85.4 5.0 %collective-permute-start.25 = (f32[128,256]{1,0:T(8,128)S(1)}, f32[128,256]{1,0:T(8,128)S(1)}, u32[]{:S(2)}, u32[]{:S(2)}) collective-permute-start(f32[128,256]{1,0:T(8,128)S(1)} %slice.81), channel_id=1, source_target_pairs={{0,4},{8,0},{16,8},{24,16},{28,24},{20,28},{12,20},{4,12},{1,5},{9... | collective-permute-start | bytes 393224 | tf_op jit(solution)/shard_map/ppermute | solution.py:280
  (6 other events, 15.1 us)
